TPU v7x, 32 devices: a whole 2x2x4 slice. The times are simulated.
32 devices in a mesh: dom: 8 (over z, y), hub: 4 (over x, core).
Axes of the slice: x: 2, y: 2, z: 4, core: 2. Of those that a mesh axis runs over, the one named last changes fastest.
Arguments:
- node_feats: bfloat16 [8, 4, 2048, 256], P('dom', 'hub'), may hold values from -6 to 6
- hub_feats: bfloat16 [1024, 256], P('hub'), may hold values from -6 to 6
- w_self: bfloat16 [256, 256], replicated, may hold values from -0.375 to 0.375
- w_neigh: bfloat16 [256, 256], replicated, may hold values from -0.375 to 0.375
- out_bias: float32 [256], replicated, may hold values from -3 to 3
- send_rows: int32 [8, 4, 8, 32], P('dom', 'hub'), may hold values from 0 to 2047, as said below
- send_counts: int32 [8, 4, 8], P('dom', 'hub'), may hold values from 0 to 32, as said below
- local_ids: int32 [8, 4, 16, 3], P('dom', 'hub'), may hold values from 0 to 15
- local_tiles: bfloat16 [8, 4, 16, 3, 128, 128], P('dom', 'hub'), may hold values from -0.5 to 0.5
- halo_ids: int32 [8, 4, 16, 2], P('dom', 'hub'), may hold values from 0 to 1
- halo_tiles: bfloat16 [8, 4, 16, 2, 128, 128], P('dom', 'hub'), may hold values from -0.5 to 0.5
- hub_ids: int32 [8, 4, 16, 2], P('dom', 'hub'), may hold values from 0 to 7
- hub_tiles: bfloat16 [8, 4, 16, 2, 128, 128], P('dom', 'hub'), may hold values from -0.5 to 0.5
- degree: int32 [8, 4, 2048], P('dom', 'hub'), may hold values from 1 to 8
- out_grad: bfloat16 [8, 4, 2048, 256], P('dom', 'hub'), may hold values from -6 to 6
Outputs:
- layer_out: bfloat16 [8, 4, 2048, 256], P('dom', 'hub')
- feats_grad: bfloat16 [8, 4, 2048, 256], P('dom', 'hub')
- grad_self: float32 [256, 256], replicated
- grad_neigh: float32 [256, 256], replicated
- grad_bias: float32 [256], replicated
- hub_grads: float32 [1024, 256], P('hub')
Inputs may be any that keep to these rules, and one draw needn't show every extreme that they name: `send_rows`: entry [p, h, a, s] is a row of partition (p, h) that it sends to partition (a, h) in slot s; only the first send_counts[p, h, a] slots of a list are used. `send_counts`: a partition sends nothing to itself; each partition sends 32 rows to at least one peer and receives 32 rows from at least one peer.
All inputs are finite; a program needn't handle non-finite values.
Results may differ from a plain program's by a relative error of at most 0.0056.
Values may be sent and summed in bfloat16 or wider, within the bound.
A program may use at most 128 MiB of HBM per device.

v0:
```python
import math

import jax
import jax.numpy as jnp
from jax import lax
from jax.sharding import PartitionSpec as P


def block_apply(tile_set, sources):
    return jnp.einsum("bkij,bkjf->bif", tile_set, sources, preferred_element_type=jnp.float32)


def block_spread(tile_set, grad_blocks):
    return jnp.einsum("bkij,bif->bkjf", tile_set, grad_blocks, preferred_element_type=jnp.float32)


def silu_slope(preact):
    sigmoid = jax.nn.sigmoid(preact)
    return sigmoid * (1.0 + preact * (1.0 - sigmoid))


def collect_blocks(pieces, index_table, block_total):
    flat_parts = pieces.reshape(
        pieces.shape[0] * pieces.shape[1], pieces.shape[2] * pieces.shape[3]
    )
    wanted = lax.broadcasted_iota(jnp.int32, (block_total, 1), 0)
    onehot = (index_table.reshape(1, -1) == wanted).astype(jnp.float32)
    return jnp.dot(
        onehot, flat_parts, precision=lax.Precision.HIGHEST, preferred_element_type=jnp.float32
    )


def body(
    node_feats,
    hub_feats,
    w_self,
    w_neigh,
    out_bias,
    send_rows,
    send_counts,
    local_ids,
    local_tiles,
    halo_ids,
    halo_tiles,
    hub_ids,
    hub_tiles,
    degree,
    out_grad,
):
    row_count = node_feats.shape[2]
    feat_width = node_feats.shape[3]
    tile_size = local_tiles.shape[-1]
    block_count = row_count // tile_size
    peer_count = lax.axis_size("dom")
    loop_count = lax.axis_size("hub")
    features = node_feats.reshape(row_count, feat_width)
    send_index = send_rows.reshape(peer_count, -1)
    slot_count = send_index.shape[1]
    send_live = lax.broadcasted_iota(jnp.int32, (peer_count, slot_count), 1) < send_counts.reshape(
        peer_count, 1
    )
    outgoing = jnp.where(send_live[:, :, None], features[send_index], jnp.zeros((), features.dtype))
    halo_rows = lax.all_to_all(outgoing, "dom", split_axis=0, concat_axis=0, tiled=True)
    hub_all = lax.all_gather(hub_feats, "hub", axis=0, tiled=True)
    local_index = local_ids[0, 0]
    local_tile = local_tiles[0, 0]
    halo_index = halo_ids[0, 0]
    halo_tile = halo_tiles[0, 0]
    hub_index = hub_ids[0, 0]
    hub_tile = hub_tiles[0, 0]
    summed = block_apply(
        local_tile, features.reshape(block_count, tile_size, feat_width)[local_index]
    )
    summed = summed + block_apply(
        halo_tile, halo_rows.reshape(-1, tile_size, feat_width)[halo_index]
    )
    summed = summed + block_apply(hub_tile, hub_all.reshape(-1, tile_size, feat_width)[hub_index])
    row_scale = 1.0 / degree.reshape(row_count).astype(jnp.float32)
    aggregate = (summed.reshape(row_count, feat_width) * row_scale[:, None]).astype(jnp.bfloat16)
    preact = (
        jnp.dot(features, w_self, preferred_element_type=jnp.float32)
        + jnp.dot(aggregate, w_neigh, preferred_element_type=jnp.float32)
        + out_bias
    )
    layer_rows = jax.nn.silu(preact).astype(jnp.bfloat16)
    grad_pre = (
        out_grad.reshape(row_count, feat_width).astype(jnp.float32) * silu_slope(preact)
    ).astype(jnp.bfloat16)
    contract_rows = (((0,), (0,)), ((), ()))
    contract_cols = (((1,), (1,)), ((), ()))
    part_self = lax.dot_general(
        features, grad_pre, contract_rows, preferred_element_type=jnp.float32
    )
    part_neigh = lax.dot_general(
        aggregate, grad_pre, contract_rows, preferred_element_type=jnp.float32
    )
    part_bias = jnp.sum(grad_pre.astype(jnp.float32), axis=0)
    total_self, total_neigh, total_bias = lax.psum(
        (part_self, part_neigh, part_bias), ("dom", "hub")
    )
    factor = 1.0 / math.sqrt(row_count * peer_count * loop_count)
    direct = lax.dot_general(grad_pre, w_self, contract_cols, preferred_element_type=jnp.float32)
    grad_scaled = lax.dot_general(
        grad_pre, w_neigh, contract_cols, preferred_element_type=jnp.float32
    )
    grad_scaled = (
        (grad_scaled * row_scale[:, None])
        .astype(jnp.bfloat16)
        .reshape(block_count, tile_size, feat_width)
    )
    halo_back = collect_blocks(
        block_spread(halo_tile, grad_scaled), halo_index, peer_count * slot_count // tile_size
    )
    returned = lax.all_to_all(
        halo_back.reshape(peer_count, slot_count, feat_width),
        "dom",
        split_axis=0,
        concat_axis=0,
        tiled=True,
    )
    local_back = collect_blocks(block_spread(local_tile, grad_scaled), local_index, block_count)
    own_grad = direct + local_back.reshape(row_count, feat_width)
    returned = jnp.where(send_live[:, :, None], returned, jnp.zeros((), returned.dtype))
    own_grad = own_grad.at[send_index.reshape(-1)].add(returned.reshape(-1, feat_width))
    hub_pieces = block_spread(hub_tile, grad_scaled)
    hub_dev_rows = hub_feats.shape[0]
    own_blocks = hub_dev_rows // tile_size
    full_sum = collect_blocks(hub_pieces, hub_index, own_blocks * loop_count)
    full_sum = lax.psum(full_sum, ("dom", "hub"))
    my_share = lax.dynamic_slice_in_dim(full_sum, lax.axis_index("hub") * own_blocks, own_blocks, 0)
    hub_grads = my_share.reshape(hub_dev_rows, feat_width)
    return (
        layer_rows.reshape(node_feats.shape),
        own_grad.astype(jnp.bfloat16).reshape(node_feats.shape),
        total_self * factor,
        total_neigh * factor,
        total_bias * factor,
        hub_grads,
    )


def solution(mesh):
    placed = (
        P("dom", "hub", None, None),
        P("hub", None),
        P(),
        P(),
        P(),
        P("dom", "hub", None, None),
        P("dom", "hub", None),
        P("dom", "hub", None, None),
        P("dom", "hub", None, None, None, None),
        P("dom", "hub", None, None),
        P("dom", "hub", None, None, None, None),
        P("dom", "hub", None, None),
        P("dom", "hub", None, None, None, None),
        P("dom", "hub", None),
        P("dom", "hub", None, None),
    )
    return jax.shard_map(
        body,
        mesh=mesh,
        in_specs=placed,
        out_specs=(
            P("dom", "hub", None, None),
            P("dom", "hub", None, None),
            P(),
            P(),
            P(),
            P("hub", None),
        ),
        check_vma=False,
    )
```

profile of v0, /device:TPU:0, one launch (start us, length us, event | category | flops | bytes accessed | tf_op | source)
XLA Modules:
  0.0 287.2 jit_solution(3315615849919298533)
XLA Ops:
  7.2 0.9 iota_compare_fusion.3
  8.1 0.7 compare_select_fusion
  8.9 2.3 gather_fusion.1
  11.2 0.8 broadcast_select_fusion.1
  12.0 7.3 %all-to-all-start = ((bf16[8,32,256]{2,1,0:T(8,128)(2,1)}), bf16[8,32,256]{2,1,0:T(8,128)(2,1)S(1)}, u32[]{:S(2)}, u32[]{:S(2)}) async-start(bf16[8,32,256]{2,1,0:T(8,128)(2,1)} %broadcast_select_fusion.1), calls=%async_computation | async-start | bytes 262144 | tf_op jit(solution)/shard_map/all_to_all | solution.py:63
  19.2 0.7 compare_select_fusion.4
  19.9 0.7 compare_select_fusion.3
  20.6 0.7 compare_select_fusion.1
  21.8 0.7 convert_divide_fusion
  22.6 7.4 %all_gather.3 = bf16[1024,256]{1,0:T(8,128)(2,1)S(1)} all-gather(bf16[256,256]{1,0:T(8,128)(2,1)} %param.16), channel_id=1, replica_groups=mesh['dom'=8,'hub'=4] {'hub'}, dimensions={0}, use_global_device_ids=true | all-gather | bytes 655360 | tf_op jit(solution)/shard_map/all_gather | solution.py:64
  29.9 1.8 fusion.22
  31.7 2.5 gather_fusion
  34.3 4.0 %fusion.5 = f32[16,256,128,1]{1,2,3,0:T(8,128)} fusion(bf16[16,3,128,256]{3,2,1,0:T(8,128)(2,1)} %bitcast.139, bf16[1,1,16,3,128,128]{5,4,3,2,1,0:T(8,128)(2,1)S(1)} %copy-done), kind=kOutput, calls=%fused_computation.23 | convolution fusion | flops 402653184 | bytes 6815744 | tf_op jit(solution)/shard_map/bkij,bkjf->bif/dot_general | solution.py:10
  38.9 2.0 gather_fusion.3
  40.9 2.0 gather_fusion.2
  43.0 2.6 fusion.10
  45.5 0.6 copy-done.6
  46.4 0.6 bitcast_add_fusion
  47.1 0.3 fusion.3
  47.6 1.1 copy-done.9
  48.7 2.2 convert_reduce_fusion
  50.9 1.2 fusion.25
  52.2 1.2 convolution_bitcast_fusion.3
  53.3 0.5 fusion.1
  53.8 2.7 convolution_bitcast_fusion.1
  56.6 2.8 convolution_bitcast_fusion.2
  59.4 3.7 %convolution_bitcast_fusion = f32[16,3,128,256]{2,3,1,0:T(8,128)} fusion(bf16[16,128,256,1]{2,1,3,0:T(8,128)(2,1)S(1)} %bitcast.137, bf16[1,1,16,3,128,128]{5,4,3,2,1,0:T(8,128)(2,1)S(1)} %copy-done), kind=kOutput, calls=%fused_computation.9 | convolution fusion | flops 402653184 | bytes 8912896 | tf_op jit(solution)/shard_map/bkij,bif->bkjf/dot_general | solution.py:14
  63.1 40.2 %psum.30 = f32[256]{0:T(256)S(1)} all-reduce(f32[256]{0:T(256)S(1)} %get-tuple-element.21), channel_id=1, replica_groups=mesh['dom'=8,'hub'=4] {'dom','hub'}, use_global_device_ids=true, to_apply=%region_4.5 | all-reduce | flops 256 | bytes 2048 | tf_op jit(solution)/shard_map/psum | solution.py:98
  103.3 5.5 %copy.63 = f32[4,8,128,256]{3,1,2,0:T(8,128)} copy(f32[4,8,128,256]{2,3,1,0:T(8,128)} %bitcast.133) | data formatting | bytes 8388608
  108.8 5.5 %copy.62 = f32[4,8,128,256]{3,1,2,0:T(8,128)} copy(f32[4,8,128,256]{2,3,1,0:T(8,128)} %bitcast.132) | data formatting | bytes 8388608
  114.3 3.6 %fusion.17 = f32[2,32768]{1,0:T(2,128)S(1)} fusion(f32[32,32768]{1,0:T(8,128)} %bitcast.134, s32[32]{0:T(128)S(1)} %eq.49), kind=kOutput, calls=%fused_computation.54 | convolution fusion | flops 25165888 | bytes 4456576 | tf_op jit(solution)/shard_map/dot_general | solution.py:28
  117.9 0.9 reshape.247
  118.8 5.3 %all-to-all-start.1 = ((f32[8,32,256]{2,1,0:T(8,128)}), f32[8,32,256]{2,1,0:T(8,128)S(1)}, u32[]{:S(2)}, u32[]{:S(2)}) async-start(f32[8,32,256]{2,1,0:T(8,128)} %reshape.247), calls=%async_computation.1 | async-start | bytes 524288 | tf_op jit(solution)/shard_map/all_to_all | solution.py:114
  124.1 6.6 %copy.61 = f32[6,8,128,256]{3,1,2,0:T(8,128)} copy(f32[6,8,128,256]{2,3,1,0:T(8,128)} %bitcast.129) | data formatting | bytes 12582912
  130.7 4.2 %fusion.13 = f32[16,32768]{1,0:T(8,128)S(1)} fusion(f32[48,32768]{1,0:T(8,128)} %bitcast.130, s32[48]{0:T(128)S(1)} %eq.45), kind=kOutput, calls=%fused_computation.41 | convolution fusion | flops 301990656 | bytes 8388800 | tf_op jit(solution)/shard_map/dot_general | solution.py:28
  134.9 1.5 reshape.245
  136.4 4.6 %fusion.15 = f32[8,32768]{1,0:T(8,128)} fusion(f32[32,32768]{1,0:T(8,128)} %bitcast.131, s32[32]{0:T(128)S(1)} %eq.53), kind=kOutput, calls=%fused_computation.50 | convolution fusion | flops 100663552 | bytes 5243008 | tf_op jit(solution)/shard_map/dot_general | solution.py:28
  141.1 1.2 copy-done.4
  142.3 3.4 %convolution_add_fusion = f32[2048,256]{1,0:T(8,128)} fusion(f32[2048,256]{1,0:T(8,128)} %reshape.245, bf16[2048,256]{1,0:T(8,128)(2,1)S(1)} %copy-done.4, bf16[256,256]{1,0:T(8,128)(2,1)S(1)} %copy-done.10), kind=kOutput, calls=%fused_computation.6 | convolution fusion | flops 268959744 | bytes 5373952 | tf_op jit(solution)/shard_map/dot_general | solution.py:102
  145.6 0.6 broadcast_multiply_fusion.2
  146.3 4.7 %scatter_fusion = f32[2048,256]{1,0:T(8,128)} fusion(f32[2048,256]{1,0:T(8,128)} %convolution_add_fusion, s32[256]{0:T(256)S(1)} %bitcast.146, f32[256,256]{1,0:T(8,128)S(1)} %bitcast.142), kind=kCustom, calls=%fused_computation.4 | custom fusion | flops 65536 | bytes 787456 | tf_op jit(solution)/shard_map/scatter-add | solution.py:124
  151.0 2.8 convert_bitcast_fusion
  153.8 121.6 %all-reduce.3.cloned.1.call-done = (f32[256,256]{0,1:T(8,128)}, f32[256,256]{0,1:T(8,128)}, f32[8,32768]{1,0:T(8,128)}) async-done(((f32[256,256]{0,1:T(8,128)}, f32[256,256]{0,1:T(8,128)}, f32[8,32768]{1,0:T(8,128)}), (f32[256,256]{0,1:T(8,128)}, f32[256,256]{0,1:T(8,128)}, f32[8,32768]{1,0:T(8,128)})) %all-reduce.3.cloned.1.call-update) | async-done | bytes 1572880 | tf_op jit(solution)/shard_map/psum | solution.py:98
  275.4 1.1 broadcast_multiply_fusion
  276.5 0.8 copy.47
  277.3 1.3 constant_dynamic-slice_fusion
  278.6 0.9 reshape.251
  279.6 0.8 copy.46
  (57 shorter events, 1.9 us)
Async XLA Ops:
  7.2 27.1 %copy-start = (bf16[1,1,16,3,128,128]{5,4,3,2,1,0:T(8,128)(2,1)S(1)}, bf16[1,1,16,3,128,128]{5,4,3,2,1,0:T(8,128)(2,1)}, u32[]{:S(2)}) copy-start(bf16[1,1,16,3,128,128]{5,4,3,2,1,0:T(8,128)(2,1)} %param.23) | copy-start | bytes 4718596
  7.2 22.8 %copy-start.2 = (bf16[1,1,2048,256]{3,2,1,0:T(8,128)(2,1)S(1)}, bf16[1,1,2048,256]{3,2,1,0:T(8,128)(2,1)}, u32[]{:S(2)}) copy-start(bf16[1,1,2048,256]{3,2,1,0:T(8,128)(2,1)} %param.15) | copy-start | bytes 3145732
  7.2 22.7 %copy-start.10 = (bf16[256,256]{1,0:T(8,128)(2,1)S(1)}, bf16[256,256]{1,0:T(8,128)(2,1)}, u32[]{:S(2)}) copy-start(bf16[256,256]{1,0:T(8,128)(2,1)} %param.17) | copy-start | bytes 393220
  12.0 29.0 %all-to-all-start = ((bf16[8,32,256]{2,1,0:T(8,128)(2,1)}), bf16[8,32,256]{2,1,0:T(8,128)(2,1)S(1)}, u32[]{:S(2)}, u32[]{:S(2)}) async-start(bf16[8,32,256]{2,1,0:T(8,128)(2,1)} %broadcast_select_fusion.1), calls=%async_computation | async-start | bytes 262144 | tf_op jit(solution)/shard_map/all_to_all | solution.py:63
  34.3 4.0 %copy-start.12 = (s32[1,1,8,32]{3,2,1,0:T(8,128)S(1)}, s32[1,1,8,32]{3,2,1,0:T(8,128)}, u32[]{:S(2)}) copy-start(s32[1,1,8,32]{3,2,1,0:T(8,128)} %param.20) | copy-start | bytes 3076
  34.3 4.1 %copy-start.13 = (s32[1,1,16,3]{2,1,3,0:T(1,128)S(1)}, s32[1,1,16,3]{2,1,3,0:T(1,128)}, u32[]{:S(2)}) copy-start(s32[1,1,16,3]{2,1,3,0:T(1,128)} %param.22) | copy-start | bytes 580
  34.3 4.2 %copy-start.14 = (s32[1,1,16,2]{2,3,1,0:T(2,128)S(1)}, s32[1,1,16,2]{2,3,1,0:T(2,128)}, u32[]{:S(2)}) copy-start(s32[1,1,16,2]{2,3,1,0:T(2,128)} %param.24) | copy-start | bytes 388
  34.3 4.2 %copy-start.15 = (s32[1,1,16,2]{2,3,1,0:T(2,128)S(1)}, s32[1,1,16,2]{2,3,1,0:T(2,128)}, u32[]{:S(2)}) copy-start(s32[1,1,16,2]{2,3,1,0:T(2,128)} %param.26) | copy-start | bytes 388
  42.9 2.6 copy-start.5
  42.9 3.2 %copy-start.6 = (bf16[32,128,256]{2,1,0:T(8,128)(2,1)S(1)}, bf16[32,128,256]{2,1,0:T(8,128)(2,1)}, u32[]{:S(2)}) copy-start(bf16[32,128,256]{2,1,0:T(8,128)(2,1)} %gather_fusion.3) | copy-start | bytes 6291460
  43.0 3.4 %copy-start.7 = (bf16[1,1,16,2,128,128]{5,4,3,2,1,0:T(8,128)(2,1)S(1)}, bf16[1,1,16,2,128,128]{5,4,3,2,1,0:T(8,128)(2,1)}, u32[]{:S(2)}) copy-start(bf16[1,1,16,2,128,128]{5,4,3,2,1,0:T(8,128)(2,1)} %param.27) | copy-start | bytes 3145732
  46.4 1.2 copy-start.16
  47.0 1.7 copy-start.9
  47.0 1.7 copy-start.11
  47.0 1.7 copy-start.17
  50.9 2.4 copy-start.3
  53.8 2.7 copy-start.8
  118.8 27.4 %all-to-all-start.1 = ((f32[8,32,256]{2,1,0:T(8,128)}), f32[8,32,256]{2,1,0:T(8,128)S(1)}, u32[]{:S(2)}, u32[]{:S(2)}) async-start(f32[8,32,256]{2,1,0:T(8,128)} %reshape.247), calls=%async_computation.1 | async-start | bytes 524288 | tf_op jit(solution)/shard_map/all_to_all | solution.py:114
  124.1 151.3 %all-reduce.3.cloned.1.call-start = ((), (), s32[]{:S(2)}) async-start(), calls=%async_computation.2 | async-start | bytes 3145728 | tf_op jit(solution)/shard_map/psum | solution.py:98
  141.0 1.2 copy-start.4
  151.0 129.4 %copy-start.1 = (bf16[1,1,16,3,128,128]{5,4,3,2,1,0:T(8,128)(2,1)S(1)}, bf16[1,1,16,3,128,128]{5,4,3,2,1,0:T(8,128)(2,1)}, u32[]{:S(2)}) copy-start(bf16[1,1,16,3,128,128]{5,4,3,2,1,0:T(8,128)(2,1)} %param.23) | copy-start | bytes 4718596
Sparse Core Ops, SparseCore 0:
  141.2 134.1 all-reduce.2
where the time goes:
time: 288 us; the launch traced here: 287 us
  waiting for transfers between devices  122 us (42%)
  blocking collectives  47.6 us (17%)
  matrix products  39 us (14%)
  local copies, waits for them, and re-layouts  37.5 us (13%)
  other arithmetic  14.7 us (5%)
  between operations  14.2 us (5%)
  starting transfers between devices  12.6 us (4%)
    psum x1, waiting for transfers between devices, body(): lax.psum((part_self, part_neigh, part_bias), ('dom', 'hub'))  122 us
    psum x1, blocking collectives, body(): lax.psum((part_self, part_neigh, part_bias), ('dom', 'hub'))  40.2 us
    unnamed x44, local copies, waits for them, and re-layouts  22.9 us
    dot_general x3, matrix products, collect_blocks(): jnp.dot(onehot, flat_parts, precision=lax.Precision.HIGHEST, preferred_el...  12.4 us
    dot_general x3, matrix products, block_spread(): jnp.einsum('bkij,bif->bkjf', tile_set, grad_blocks, preferred_element_typ...  9.24 us
    all_gather x1, blocking collectives, body(): hub_all = lax.all_gather(hub_feats, 'hub', axis=0, tiled=True)  7.38 us
    all_to_all x1, starting transfers between devices, body(): lax.all_to_all(outgoing, 'dom', split_axis=0, concat_axis=0, tiled=True)  7.28 us
    dot_general x3, matrix products, block_apply(): jnp.einsum('bkij,bkjf->bif', tile_set, sources, preferred_element_type=jn...  7.16 us
  transfers between devices with their start and end apart: 3, of which 1 were waited for; matrix products, arithmetic and copies ran while one was open for 15% of the time, Pallas kernels for 0%

commit v1 on v0

v1 whole, which is shorter than its diff:
```python
import functools
import math

import jax
import jax.numpy as jnp
from jax import lax
from jax.experimental import pallas as pl
from jax.experimental.pallas import tpu as pltpu
from jax.sharding import PartitionSpec as P

F32 = jnp.float32
BF16 = jnp.bfloat16
MESH = pl.DeviceIdType.MESH
VMEM_SPEC = pl.BlockSpec(memory_space=pltpu.VMEM)
VMEM_LIMIT = 48 * 1024 * 1024


def rows_at(index, size):
    return pl.ds(pl.multiple_of(index * size, size), size)


def greet(dom_size, hub_size, dom, hub):
    barrier = pltpu.get_barrier_semaphore()
    for off in range(1, hub_size):
        pl.semaphore_signal(
            barrier, inc=1, device_id=(dom, lax.rem(hub + off, hub_size)), device_id_type=MESH
        )
    for off in range(1, dom_size):
        pl.semaphore_signal(
            barrier, inc=1, device_id=(lax.rem(dom + off, dom_size), hub), device_id_type=MESH
        )
    return barrier


def remote(src, dst, send, recv, dom, hub):
    return pltpu.make_async_remote_copy(
        src_ref=src,
        dst_ref=dst,
        send_sem=send,
        recv_sem=recv,
        device_id=(dom, hub),
        device_id_type=MESH,
    )


def exchange_kernel(
    dom_size,
    hub_size,
    index_ref,
    feats_ref,
    hub_ref,
    halo_ref,
    hub_all_ref,
    outgoing,
    hub_send,
    hub_recv,
    dom_send,
    dom_recv,
):
    dom = lax.axis_index("dom")
    hub = lax.axis_index("hub")
    barrier = greet(dom_size, hub_size, dom, hub)
    row_count = feats_ref.shape[0]
    hub_rows = hub_ref.shape[0]
    slots = index_ref.shape[1]
    cap = slots // dom_size
    hub_all_ref[rows_at(hub, hub_rows), :] = hub_ref[...]
    pl.semaphore_wait(barrier, hub_size + dom_size - 2)
    copies = []
    for off in range(1, hub_size):
        copies.append(
            remote(
                hub_ref,
                hub_all_ref.at[rows_at(hub, hub_rows)],
                hub_send.at[off],
                hub_recv.at[off],
                dom,
                lax.rem(hub + off, hub_size),
            )
        )
        copies[-1].start()
    for part in range(slots // 128):
        wanted = jnp.broadcast_to(
            index_ref[:, part * 128 : (part + 1) * 128].astype(F32), (128, 128)
        ).T
        lane = lax.broadcasted_iota(jnp.int32, (128, 128), 1).astype(F32)
        onehot = jnp.concatenate(
            [
                (wanted == lane + float(start)).astype(F32).astype(BF16)
                for start in range(0, row_count, 128)
            ],
            axis=1,
        )
        outgoing[part * 128 : (part + 1) * 128, :] = jnp.dot(
            onehot, feats_ref[...], preferred_element_type=F32
        ).astype(BF16)
    for off in range(1, dom_size):
        target = lax.rem(dom + off, dom_size)
        copies.append(
            remote(
                outgoing.at[rows_at(target, cap)],
                halo_ref.at[rows_at(dom, cap)],
                dom_send.at[off],
                dom_recv.at[off],
                target,
                hub,
            )
        )
        copies[-1].start()
    halo_ref[rows_at(dom, cap), :] = outgoing[rows_at(dom, cap), :]
    for copy in copies:
        copy.wait()


def layer_kernel(
    span,
    hub_size,
    weight_rows,
    local_ids,
    halo_ids,
    hub_ids,
    feats_ref,
    halo_ref,
    hub_ref,
    local_tiles,
    halo_tiles,
    hub_tiles,
    degree_ref,
    out_grad_ref,
    w_self_ref,
    w_neigh_ref,
    bias_ref,
    layer_ref,
    own_ref,
    halo_back_ref,
    payload_ref,
    bias_part_ref,
    halo_acc,
    hub_acc,
    weight_acc,
    bias_acc,
):
    step = pl.program_id(0)
    width = feats_ref.shape[1]

    @pl.when(step == 0)
    def _():
        own_ref[...] = jnp.zeros_like(own_ref)
        halo_acc[...] = jnp.zeros_like(halo_acc)
        hub_acc[...] = jnp.zeros_like(hub_acc)
        weight_acc[...] = jnp.zeros_like(weight_acc)
        bias_acc[...] = jnp.zeros_like(bias_acc)

    groups = (
        (local_ids, local_tiles, feats_ref, own_ref),
        (halo_ids, halo_tiles, halo_ref, halo_acc),
        (hub_ids, hub_tiles, hub_ref, hub_acc),
    )
    features = feats_ref[rows_at(step, span * 128), :]
    scales = []
    sums = []
    for sub in range(span):
        block = step * span + sub
        scale = 1.0 / degree_ref[pl.ds(block, 1), :].astype(F32)
        scale = jnp.broadcast_to(scale, (128, 128)).T
        scales.append(jnp.concatenate([scale] * (width // 128), axis=1))
        tiles = []
        sources = []
        for ids, tile_ref, source_ref, _ in groups:
            for k in range(tile_ref.shape[1]):
                tiles.append(tile_ref[sub, k])
                sources.append(source_ref[rows_at(ids[block, k], 128), :])
        total = jnp.dot(
            jnp.concatenate(tiles, axis=1),
            jnp.concatenate(sources, axis=0),
            preferred_element_type=F32,
        )
        sums.append((total * scales[-1]).astype(BF16))
    aggregate = jnp.concatenate(sums, axis=0)
    preact = (
        jnp.dot(features, w_self_ref[...], preferred_element_type=F32)
        + jnp.dot(aggregate, w_neigh_ref[...], preferred_element_type=F32)
        + bias_ref[...]
    )
    sigmoid = 1.0 / (1.0 + jnp.exp(-preact))
    layer_ref[...] = (preact * sigmoid).astype(BF16)
    grad_wide = out_grad_ref[...].astype(F32) * (sigmoid * (1.0 + preact * (1.0 - sigmoid)))
    grad_pre = grad_wide.astype(BF16)
    bias_acc[...] += jnp.sum(
        grad_pre.astype(F32).reshape(span * 16, 8, width), axis=0
    )
    contract_rows = (((0,), (0,)), ((), ()))
    contract_cols = (((1,), (1,)), ((), ()))
    weight_acc[...] += lax.dot_general(
        jnp.concatenate([features, aggregate], axis=1),
        grad_pre,
        contract_rows,
        preferred_element_type=F32,
    )
    own_ref[rows_at(step, span * 128), :] += lax.dot_general(
        grad_pre, w_self_ref[...], contract_cols, preferred_element_type=F32
    )
    back = lax.dot_general(grad_pre, w_neigh_ref[...], contract_cols, preferred_element_type=F32)
    for sub in range(span):
        block = step * span + sub
        scaled = (back[sub * 128 : (sub + 1) * 128, :] * scales[sub]).astype(BF16)
        for ids, tile_ref, _, acc_ref in groups:
            for k in range(tile_ref.shape[1]):
                acc_ref[rows_at(ids[block, k], 128), :] += lax.dot_general(
                    tile_ref[sub, k], scaled, contract_rows, preferred_element_type=F32
                )

    @pl.when(step == pl.num_programs(0) - 1)
    def _():
        halo_back_ref[...] = halo_acc[...].astype(BF16)
        hub_rows = hub_acc.shape[0] // hub_size
        chunk = payload_ref.shape[1]
        for peer in range(hub_size):
            payload_ref[peer, :weight_rows, :] = weight_acc[
                peer * weight_rows : (peer + 1) * weight_rows, :
            ].astype(BF16)
            payload_ref[peer, weight_rows : weight_rows + hub_rows, :] = hub_acc[
                peer * hub_rows : (peer + 1) * hub_rows, :
            ].astype(BF16)
            if weight_rows + hub_rows < chunk:
                payload_ref[peer, weight_rows + hub_rows :, :] = jnp.zeros(
                    (chunk - weight_rows - hub_rows, width), BF16
                )
        bias_part_ref[...] = bias_acc[...]


def reduce_kernel(
    dom_size,
    hub_size,
    weight_rows,
    factor,
    index_ref,
    own_ref,
    halo_back_ref,
    payload_ref,
    bias_part_ref,
    feats_grad_ref,
    self_ref,
    neigh_ref,
    bias_out_ref,
    hub_out_ref,
    returned,
    hub_land,
    partial,
    dom_land,
    gathered,
    weights,
    bias_hub,
    bias_dom,
    hub_send,
    hub_recv,
    bias_hub_send,
    bias_hub_recv,
    back_send,
    back_recv,
    dom_send,
    dom_recv,
    bias_dom_send,
    bias_dom_recv,
    gather_send,
    gather_recv,
    weight_send,
    weight_recv,
):
    dom = lax.axis_index("dom")
    hub = lax.axis_index("hub")
    slots = index_ref.shape[1]
    cap = slots // dom_size
    chunk = payload_ref.shape[1]
    piece = chunk // dom_size
    width = own_ref.shape[1]
    barrier = greet(dom_size, hub_size, dom, hub)
    bias_hub[hub] = bias_part_ref[...]
    returned[rows_at(dom, cap), :] = halo_back_ref[rows_at(dom, cap), :]
    pl.semaphore_wait(barrier, hub_size + dom_size - 2)

    hub_copies = []
    for off in range(1, hub_size):
        target = lax.rem(hub + off, hub_size)
        hub_copies.append(
            remote(
                payload_ref.at[target],
                hub_land.at[off],
                hub_send.at[off],
                hub_recv.at[off],
                dom,
                target,
            )
        )
        hub_copies.append(
            remote(
                bias_part_ref,
                bias_hub.at[hub],
                bias_hub_send.at[off],
                bias_hub_recv.at[off],
                dom,
                target,
            )
        )
    for copy in hub_copies:
        copy.start()
    back_copies = []
    for off in range(1, dom_size):
        target = lax.rem(dom + off, dom_size)
        back_copies.append(
            remote(
                halo_back_ref.at[rows_at(target, cap)],
                returned.at[rows_at(dom, cap)],
                back_send.at[off],
                back_recv.at[off],
                target,
                hub,
            )
        )
        back_copies[-1].start()
    for copy in hub_copies:
        copy.wait()
    total = payload_ref[hub].astype(F32)
    for off in range(1, hub_size):
        total = total + hub_land[off].astype(F32)
    partial[...] = total.astype(BF16)
    bias_total = bias_hub[0]
    for peer in range(1, hub_size):
        bias_total = bias_total + bias_hub[peer]
    bias_dom[dom] = bias_total

    dom_copies = []
    for off in range(1, dom_size):
        target = lax.rem(dom + off, dom_size)
        dom_copies.append(
            remote(
                partial.at[rows_at(target, piece)],
                dom_land.at[off],
                dom_send.at[off],
                dom_recv.at[off],
                target,
                hub,
            )
        )
        dom_copies.append(
            remote(
                bias_dom.at[dom],
                bias_dom.at[dom],
                bias_dom_send.at[off],
                bias_dom_recv.at[off],
                target,
                hub,
            )
        )
    for copy in dom_copies:
        copy.start()
    for copy in dom_copies:
        copy.wait()
    total = partial[rows_at(dom, piece), :].astype(F32)
    for off in range(1, dom_size):
        total = total + dom_land[off].astype(F32)
    gathered[rows_at(dom, piece), :] = total.astype(BF16)
    gather_copies = []
    for off in range(1, dom_size):
        gather_copies.append(
            remote(
                gathered.at[rows_at(dom, piece)],
                gathered.at[rows_at(dom, piece)],
                gather_send.at[off],
                gather_recv.at[off],
                lax.rem(dom + off, dom_size),
                hub,
            )
        )
        gather_copies[-1].start()
    bias_total = bias_dom[0]
    for peer in range(1, dom_size):
        bias_total = bias_total + bias_dom[peer]
    bias_out_ref[...] = jnp.sum(bias_total, axis=0, keepdims=True) * factor

    for copy in back_copies:
        copy.wait()
    row_count = own_ref.shape[0]

    def add_back(step, carry):
        rows = rows_at(step, 256)
        row = lax.broadcasted_iota(jnp.int32, (256, slots), 0) + step * 256
        onehot = (row == index_ref[...]).astype(F32).astype(BF16)
        feats_grad_ref[rows, :] = (
            own_ref[rows, :] + jnp.dot(onehot, returned[...], preferred_element_type=F32)
        ).astype(BF16)
        return carry

    lax.fori_loop(0, row_count // 256, add_back, 0)

    for copy in gather_copies:
        copy.wait()
    weight_copies = []
    weights[hub] = gathered[:weight_rows, :]
    for off in range(1, hub_size):
        weight_copies.append(
            remote(
                gathered.at[pl.ds(0, weight_rows)],
                weights.at[hub],
                weight_send.at[off],
                weight_recv.at[off],
                dom,
                lax.rem(hub + off, hub_size),
            )
        )
        weight_copies[-1].start()
    hub_rows = hub_out_ref.shape[0]
    hub_out_ref[...] = gathered[weight_rows : weight_rows + hub_rows, :].astype(F32)
    for copy in weight_copies:
        copy.wait()
    half = hub_size // 2
    self_ref[...] = weights[:half].reshape(width, width).astype(F32) * factor
    neigh_ref[...] = weights[half:].reshape(width, width).astype(F32) * factor


def body(
    node_feats,
    hub_feats,
    w_self,
    w_neigh,
    out_bias,
    send_rows,
    send_counts,
    local_ids,
    local_tiles,
    halo_ids,
    halo_tiles,
    hub_ids,
    hub_tiles,
    degree,
    out_grad,
):
    dom_size = lax.axis_size("dom")
    hub_size = lax.axis_size("hub")
    rows, width = node_feats.shape[2:]
    tile = local_tiles.shape[-1]
    blocks = rows // tile
    cap = send_rows.shape[-1]
    slots = dom_size * cap
    hub_rows = hub_feats.shape[0]
    features = node_feats.reshape(rows, width)
    live = lax.broadcasted_iota(jnp.int32, (dom_size, cap), 1) < send_counts.reshape(dom_size, 1)
    index = jnp.where(live, send_rows.reshape(dom_size, cap), -1).reshape(1, slots)
    dma = pltpu.SemaphoreType.DMA

    halo, hub_all = pl.pallas_call(
        functools.partial(exchange_kernel, dom_size, hub_size),
        out_shape=(
            jax.ShapeDtypeStruct((slots, width), BF16),
            jax.ShapeDtypeStruct((hub_size * hub_rows, width), BF16),
        ),
        in_specs=[VMEM_SPEC] * 3,
        out_specs=(VMEM_SPEC,) * 2,
        scratch_shapes=[
            pltpu.VMEM((slots, width), BF16),
            dma((hub_size,)),
            dma((hub_size,)),
            dma((dom_size,)),
            dma((dom_size,)),
        ],
        compiler_params=pltpu.CompilerParams(
            collective_id=0, has_side_effects=True, vmem_limit_bytes=VMEM_LIMIT
        ),
        name="exchange",
    )(index, features, hub_feats)

    span = 2
    weight_rows = 2 * width // hub_size
    unit = 16 * dom_size
    chunk = (weight_rows + hub_rows + unit - 1) // unit * unit
    whole = lambda *shape: pl.BlockSpec(shape, lambda i, *_: (0,) * len(shape))
    tiles = lambda count: pl.BlockSpec((span, count, tile, tile), lambda i, *_: (i, 0, 0, 0))
    moving = pl.BlockSpec((span * tile, width), lambda i, *_: (i, 0))
    counts = (local_tiles.shape[3], halo_tiles.shape[3], hub_tiles.shape[3])
    layer_rows, own_grad, halo_back, payload, bias_part = pl.pallas_call(
        functools.partial(layer_kernel, span, hub_size, weight_rows),
        out_shape=(
            jax.ShapeDtypeStruct((rows, width), BF16),
            jax.ShapeDtypeStruct((rows, width), F32),
            jax.ShapeDtypeStruct((slots, width), BF16),
            jax.ShapeDtypeStruct((hub_size, chunk, width), BF16),
            jax.ShapeDtypeStruct((8, width), F32),
        ),
        grid_spec=pltpu.PrefetchScalarGridSpec(
            num_scalar_prefetch=3,
            grid=(blocks // span,),
            in_specs=[
                whole(rows, width),
                whole(slots, width),
                whole(hub_size * hub_rows, width),
                tiles(counts[0]),
                tiles(counts[1]),
                tiles(counts[2]),
                whole(blocks, tile),
                moving,
                whole(width, width),
                whole(width, width),
                whole(1, width),
            ],
            out_specs=(
                moving,
                whole(rows, width),
                whole(slots, width),
                whole(hub_size, chunk, width),
                whole(8, width),
            ),
            scratch_shapes=[
                pltpu.VMEM((slots, width), F32),
                pltpu.VMEM((hub_size * hub_rows, width), F32),
                pltpu.VMEM((2 * width, width), F32),
                pltpu.VMEM((8, width), F32),
            ],
        ),
        compiler_params=pltpu.CompilerParams(vmem_limit_bytes=VMEM_LIMIT),
        name="layer",
    )(
        local_ids.reshape(blocks, counts[0]),
        halo_ids.reshape(blocks, counts[1]),
        hub_ids.reshape(blocks, counts[2]),
        features,
        halo,
        hub_all,
        local_tiles.reshape(blocks, counts[0], tile, tile),
        halo_tiles.reshape(blocks, counts[1], tile, tile),
        hub_tiles.reshape(blocks, counts[2], tile, tile),
        degree.reshape(blocks, tile),
        out_grad.reshape(rows, width),
        w_self,
        w_neigh,
        out_bias.reshape(1, width),
    )

    factor = 1.0 / math.sqrt(rows * dom_size * hub_size)
    piece = chunk // dom_size
    feats_grad, grad_self, grad_neigh, grad_bias, hub_grads = pl.pallas_call(
        functools.partial(reduce_kernel, dom_size, hub_size, weight_rows, factor),
        out_shape=(
            jax.ShapeDtypeStruct((rows, width), BF16),
            jax.ShapeDtypeStruct((width, width), F32),
            jax.ShapeDtypeStruct((width, width), F32),
            jax.ShapeDtypeStruct((1, width), F32),
            jax.ShapeDtypeStruct((hub_rows, width), F32),
        ),
        in_specs=[VMEM_SPEC] * 5,
        out_specs=(VMEM_SPEC,) * 5,
        scratch_shapes=[
            pltpu.VMEM((slots, width), BF16),
            pltpu.VMEM((hub_size, chunk, width), BF16),
            pltpu.VMEM((chunk, width), BF16),
            pltpu.VMEM((dom_size, piece, width), BF16),
            pltpu.VMEM((chunk, width), BF16),
            pltpu.VMEM((hub_size, weight_rows, width), BF16),
            pltpu.VMEM((hub_size, 8, width), F32),
            pltpu.VMEM((dom_size, 8, width), F32),
            dma((hub_size,)),
            dma((hub_size,)),
            dma((hub_size,)),
            dma((hub_size,)),
            dma((dom_size,)),
            dma((dom_size,)),
            dma((dom_size,)),
            dma((dom_size,)),
            dma((dom_size,)),
            dma((dom_size,)),
            dma((dom_size,)),
            dma((dom_size,)),
            dma((hub_size,)),
            dma((hub_size,)),
        ],
        compiler_params=pltpu.CompilerParams(
            collective_id=1, has_side_effects=True, vmem_limit_bytes=VMEM_LIMIT
        ),
        name="reduce",
    )(index, own_grad, halo_back, payload, bias_part)
    return (
        layer_rows.reshape(node_feats.shape),
        feats_grad.reshape(node_feats.shape),
        grad_self,
        grad_neigh,
        grad_bias.reshape(width),
        hub_grads,
    )


def solution(mesh):
    placed = (
        P("dom", "hub", None, None),
        P("hub", None),
        P(),
        P(),
        P(),
        P("dom", "hub", None, None),
        P("dom", "hub", None),
        P("dom", "hub", None, None),
        P("dom", "hub", None, None, None, None),
        P("dom", "hub", None, None),
        P("dom", "hub", None, None, None, None),
        P("dom", "hub", None, None),
        P("dom", "hub", None, None, None, None),
        P("dom", "hub", None),
        P("dom", "hub", None, None),
    )
    return jax.shard_map(
        body,
        mesh=mesh,
        in_specs=placed,
        out_specs=(
            P("dom", "hub", None, None),
            P("dom", "hub", None, None),
            P(),
            P(),
            P(),
            P("hub", None),
        ),
        check_vma=False,
    )
```

time: 288 us -> 75.9 us (0.26)
  waiting for transfers between devices: 122 us -> 0 us
  Pallas kernels: 0 us -> 55.3 us
  blocking collectives: 47.6 us -> 0 us
  matrix products: 39 us -> 0 us
  local copies, waits for them, and re-layouts: 37.5 us -> 18.6 us
  other arithmetic: 14.7 us -> 0.74 us
  between operations: 14.2 us -> 0.67 us
  starting transfers between devices: 12.6 us -> 0 us
    psum x1 -> x0, waiting for transfers between devices: 122 us -> none  [body(): lax.psum((part_self, part_neigh, part_bias), ('dom', 'hub'))]
    pallas_call x0 -> x3, Pallas kernels: none -> 55.3 us  [the longest x1 29 us: body(): pl.pallas_call(functools.partial(reduce_kernel, dom_size, hub_size, weigh...]
    psum x1 -> x0, blocking collectives: 40.2 us -> none  [body(): lax.psum((part_self, part_neigh, part_bias), ('dom', 'hub'))]
    dot_general x15 -> x0, matrix products: 39 us -> none  [the longest x3 12.4 us: collect_blocks(): jnp.dot(onehot, flat_parts, precision=lax.Precision.HIGHEST, preferred_el...]
    all_to_all x2 -> x0, starting transfers between devices: 12.5 us -> none  [the longest x1 7.28 us: body(): lax.all_to_all(outgoing, 'dom', split_axis=0, concat_axis=0, tiled=True)]
    gather x4 -> x0, local copies, waits for them, and re-layouts: 8.94 us -> none  [the longest x1 2.55 us: body(): features.reshape(block_count, tile_size, feat_width)[local_index]]
    unnamed x44 -> x27, local copies, waits for them, and re-layouts: 22.9 us -> 15.4 us
    all_gather x1 -> x0, blocking collectives: 7.38 us -> none  [body(): hub_all = lax.all_gather(hub_feats, 'hub', axis=0, tiled=True)]
  transfers between devices with their start and end apart: 3 -> 0, of which waited for: 1 -> 0; matrix products, arithmetic and copies ran while one was open for 15% -> 0% of each run, Pallas kernels for 0% -> 0%
where the time goes in v1:
time: 75.9 us; the launch traced here: 75.3 us
  Pallas kernels  55.3 us (73%)
  local copies, waits for them, and re-layouts  18.6 us (25%)
    pallas_call x1, Pallas kernels, body(): pl.pallas_call(functools.partial(reduce_kernel, dom_size, hub_size, weigh...  29 us
    unnamed x27, local copies, waits for them, and re-layouts  15.4 us
    pallas_call x1, Pallas kernels, body(): pl.pallas_call(functools.partial(layer_kernel, span, hub_size, weight_row...  14.2 us
    pallas_call x1, Pallas kernels, body(): pl.pallas_call(functools.partial(exchange_kernel, dom_size, hub_size), ou...  12.1 us

profile of v1, /device:TPU:0, one launch (start us, length us, event | category | flops | bytes accessed | tf_op | source)
XLA Modules:
  0.0 75.3 jit_solution(3039034917863422261)
XLA Ops:
  0.6 0.8 %reshape.93 = s32[1,256]{1,0:T(1,128)S(1)} reshape(s32[1,1,8,32]{3,2,1,0:T(8,128)} %param.20) | data formatting | bytes 2048 | tf_op jit(solution)/shard_map/reshape | solution.py:448
  1.4 0.7 iota_compare_fusion
  2.1 0.1 lt.23
  2.2 0.8 %copy.24 = s32[1,1,16,3]{3,2,1,0:T(8,128)S(1)} copy(s32[1,1,16,3]{2,1,3,0:T(1,128)} %param.22) | data formatting | bytes 384 | tf_op jit(solution)/shard_map/reshape | solution.py:522
  3.0 0.8 %copy.22.halo_ids = s32[16,2]{1,0:T(8,128)S(1)} copy(s32[16,2]{0,1:T(2,128)} %bitcast.27) | data formatting | bytes 256 | tf_op jit(solution)/shard_map/reshape | solution.py:523
  3.7 0.8 %copy.23.hub_ids = s32[16,2]{1,0:T(8,128)S(1)} copy(s32[16,2]{0,1:T(2,128)} %bitcast.28) | data formatting | bytes 256 | tf_op jit(solution)/shard_map/reshape | solution.py:524
  4.5 0.0 copy-start
  4.5 1.2 %copy-done = bf16[1,1,2048,256]{3,2,1,0:T(8,128)(2,1)S(1)} copy-done((bf16[1,1,2048,256]{3,2,1,0:T(8,128)(2,1)S(1)}, bf16[1,1,2048,256]{3,2,1,0:T(8,128)(2,1)}, u32[]{:S(2)}) %copy-start) | copy-done | bytes 1048600
  5.7 0.0 copy-start.8
  5.7 0.9 %copy-done.8 = bf16[256,256]{1,0:T(8,128)(2,1)S(1)} copy-done((bf16[256,256]{1,0:T(8,128)(2,1)S(1)}, bf16[256,256]{1,0:T(8,128)(2,1)}, u32[]{:S(2)}) %copy-start.8) | copy-done | bytes 131096
  6.6 12.1 %exchange.1 = (bf16[256,256]{1,0:T(8,128)(2,1)S(1)}, bf16[1024,256]{1,0:T(8,128)(2,1)S(1)}) custom-call(s32[1,256]{1,0:T(1,128)S(1)} %broadcast_select_fusion.index_ref, bf16[2048,256]{1,0:T(8,128)(2,1)S(1)} %bitcast.16, bf16[256,256]{1,0:T(8,128)(2,1)S(1)} %copy-done.8), custom_call_target="tpu_custom_call" | custom-call | tf_op jit(solution)/shard_map/exchange/pallas_call | solution.py:451
  18.7 0.0 copy-start.1
  18.7 1.2 %copy-done.1 = bf16[1,1,2048,256]{3,2,1,0:T(8,128)(2,1)S(1)} copy-done((bf16[1,1,2048,256]{3,2,1,0:T(8,128)(2,1)S(1)}, bf16[1,1,2048,256]{3,2,1,0:T(8,128)(2,1)}, u32[]{:S(2)}) %copy-start.1) | copy-done | bytes 1048600
  20.0 0.0 copy-start.3
  20.0 1.2 %copy-done.3 = bf16[1,1,16,2,128,128]{5,4,3,2,1,0:T(8,128)(2,1)S(1)} copy-done((bf16[1,1,16,2,128,128]{5,4,3,2,1,0:T(8,128)(2,1)S(1)}, bf16[1,1,16,2,128,128]{5,4,3,2,1,0:T(8,128)(2,1)}, u32[]{:S(2)}) %copy-start.3) | copy-done | bytes 1048600
  21.2 0.0 copy-start.4
  21.2 1.2 %copy-done.4 = bf16[1,1,16,2,128,128]{5,4,3,2,1,0:T(8,128)(2,1)S(1)} copy-done((bf16[1,1,16,2,128,128]{5,4,3,2,1,0:T(8,128)(2,1)S(1)}, bf16[1,1,16,2,128,128]{5,4,3,2,1,0:T(8,128)(2,1)}, u32[]{:S(2)}) %copy-start.4) | copy-done | bytes 1048600
  22.4 0.0 copy-start.5
  22.4 1.2 %copy-done.5 = bf16[1,1,2048,256]{3,2,1,0:T(8,128)(2,1)S(1)} copy-done((bf16[1,1,2048,256]{3,2,1,0:T(8,128)(2,1)S(1)}, bf16[1,1,2048,256]{3,2,1,0:T(8,128)(2,1)}, u32[]{:S(2)}) %copy-start.5) | copy-done | bytes 1048600
  23.6 0.0 copy-start.6
  23.6 0.9 %copy-done.6 = bf16[256,256]{1,0:T(8,128)(2,1)S(1)} copy-done((bf16[256,256]{1,0:T(8,128)(2,1)S(1)}, bf16[256,256]{1,0:T(8,128)(2,1)}, u32[]{:S(2)}) %copy-start.6) | copy-done | bytes 131096
  24.5 0.0 copy-start.7
  24.5 0.9 %copy-done.7 = bf16[256,256]{1,0:T(8,128)(2,1)S(1)} copy-done((bf16[256,256]{1,0:T(8,128)(2,1)S(1)}, bf16[256,256]{1,0:T(8,128)(2,1)}, u32[]{:S(2)}) %copy-start.7) | copy-done | bytes 131096
  25.4 0.0 copy-start.9
  25.4 0.7 copy-done.9
  26.1 0.0 copy-start.10
  26.1 0.7 copy-done.10
  26.8 14.2 %layer.1 = (bf16[2048,256]{1,0:T(8,128)(2,1)}, f32[2048,256]{1,0:T(8,128)}, bf16[256,256]{1,0:T(8,128)(2,1)S(1)}, bf16[4,384,256]{2,1,0:T(8,128)(2,1)S(1)}, f32[8,256]{1,0:T(8,128)S(1)}) custom-call(s32[16,3]{1,0:T(8,128)S(1)} %bitcast.22, s32[16,2]{1,0:T(8,128)S(1)} %copy.22.halo_ids, s32[16,2]{1,0:T(8,128)S(1)} %copy.23.hub_ids, ...), custom_call_target="tpu_custom_call" | custom-call | tf_op jit(solution)/shard_map/layer/pallas_call | solution.py:480
  41.0 0.0 copy-start.2
  41.0 1.6 %copy-done.2 = f32[2048,256]{1,0:T(8,128)S(1)} copy-done((f32[2048,256]{1,0:T(8,128)S(1)}, f32[2048,256]{1,0:T(8,128)}, u32[]{:S(2)}) %copy-start.2) | copy-done | bytes 2097176
  42.6 29.0 %reduce.1 = (bf16[2048,256]{1,0:T(8,128)(2,1)S(1)}, f32[256,256]{1,0:T(8,128)S(1)}, f32[256,256]{1,0:T(8,128)S(1)}, f32[1,256]{1,0:T(1,128)S(1)}, f32[256,256]{1,0:T(8,128)S(1)}) custom-call(s32[1,256]{1,0:T(1,128)S(1)} %broadcast_select_fusion.index_ref, f32[2048,256]{1,0:T(8,128)S(1)} %copy-done.2, bf16[256,256]{1,0:T(8,128)(2,1)S(1)} %get-tuple-element.22.halo_back_ref, ...), custom_call_target="tpu_custom_call" | custom-call | tf_op jit(solution)/shard_map/reduce/pallas_call | solution.py:540
  71.6 1.0 %copy.30 = bf16[1,1,2048,256]{3,2,1,0:T(8,128)(2,1)} copy(bf16[1,1,2048,256]{3,2,1,0:T(8,128)(2,1)S(1)} %bitcast.18) | data formatting | bytes 2097152
  72.6 0.7 copy.31
  73.3 0.7 copy.32
  74.0 0.6 copy.33
  74.5 0.7 copy.34
  (1 shorter events, 0.0 us)
Async XLA Ops:
  4.5 1.2 %copy-start = (bf16[1,1,2048,256]{3,2,1,0:T(8,128)(2,1)S(1)}, bf16[1,1,2048,256]{3,2,1,0:T(8,128)(2,1)}, u32[]{:S(2)}) copy-start(bf16[1,1,2048,256]{3,2,1,0:T(8,128)(2,1)} %param.15) | copy-start | bytes 3145732
  5.7 0.9 %copy-start.8 = (bf16[256,256]{1,0:T(8,128)(2,1)S(1)}, bf16[256,256]{1,0:T(8,128)(2,1)}, u32[]{:S(2)}) copy-start(bf16[256,256]{1,0:T(8,128)(2,1)} %hub_ref.1) | copy-start | bytes 393220
  18.7 1.2 %copy-start.1 = (bf16[1,1,2048,256]{3,2,1,0:T(8,128)(2,1)S(1)}, bf16[1,1,2048,256]{3,2,1,0:T(8,128)(2,1)}, u32[]{:S(2)}) copy-start(bf16[1,1,2048,256]{3,2,1,0:T(8,128)(2,1)} %param.15) | copy-start | bytes 3145732
  20.0 1.2 %copy-start.3 = (bf16[1,1,16,2,128,128]{5,4,3,2,1,0:T(8,128)(2,1)S(1)}, bf16[1,1,16,2,128,128]{5,4,3,2,1,0:T(8,128)(2,1)}, u32[]{:S(2)}) copy-start(bf16[1,1,16,2,128,128]{5,4,3,2,1,0:T(8,128)(2,1)} %param.25) | copy-start | bytes 3145732
  21.2 1.2 %copy-start.4 = (bf16[1,1,16,2,128,128]{5,4,3,2,1,0:T(8,128)(2,1)S(1)}, bf16[1,1,16,2,128,128]{5,4,3,2,1,0:T(8,128)(2,1)}, u32[]{:S(2)}) copy-start(bf16[1,1,16,2,128,128]{5,4,3,2,1,0:T(8,128)(2,1)} %param.27) | copy-start | bytes 3145732
  22.4 1.2 %copy-start.5 = (bf16[1,1,2048,256]{3,2,1,0:T(8,128)(2,1)S(1)}, bf16[1,1,2048,256]{3,2,1,0:T(8,128)(2,1)}, u32[]{:S(2)}) copy-start(bf16[1,1,2048,256]{3,2,1,0:T(8,128)(2,1)} %param.29) | copy-start | bytes 3145732
  23.6 0.9 %copy-start.6 = (bf16[256,256]{1,0:T(8,128)(2,1)S(1)}, bf16[256,256]{1,0:T(8,128)(2,1)}, u32[]{:S(2)}) copy-start(bf16[256,256]{1,0:T(8,128)(2,1)} %w_self_ref.1) | copy-start | bytes 393220
  24.5 0.9 %copy-start.7 = (bf16[256,256]{1,0:T(8,128)(2,1)S(1)}, bf16[256,256]{1,0:T(8,128)(2,1)}, u32[]{:S(2)}) copy-start(bf16[256,256]{1,0:T(8,128)(2,1)} %w_neigh_ref.1) | copy-start | bytes 393220
  25.4 0.7 copy-start.9
  26.1 0.7 copy-start.10
  41.0 1.6 %copy-start.2 = (f32[2048,256]{1,0:T(8,128)S(1)}, f32[2048,256]{1,0:T(8,128)}, u32[]{:S(2)}) copy-start(f32[2048,256]{1,0:T(8,128)} %get-tuple-element.21.own_ref) | copy-start | bytes 6291460

commit v2 on v1

v2 whole, which is shorter than its diff:
```python
import functools
import math

import jax
import jax.numpy as jnp
from jax import lax
from jax.experimental import pallas as pl
from jax.experimental.pallas import tpu as pltpu
from jax.sharding import PartitionSpec as P

F32 = jnp.float32
BF16 = jnp.bfloat16
MESH = pl.DeviceIdType.MESH
VMEM_SPEC = pl.BlockSpec(memory_space=pltpu.VMEM)
VMEM_LIMIT = 60 * 1024 * 1024


def rows_at(index, size):
    return pl.ds(pl.multiple_of(index * size, size), size)


def greet(dom_size, hub_size, dom, hub):
    barrier = pltpu.get_barrier_semaphore()
    for off in range(1, hub_size):
        pl.semaphore_signal(
            barrier, inc=1, device_id=(dom, lax.rem(hub + off, hub_size)), device_id_type=MESH
        )
    for off in range(1, dom_size):
        pl.semaphore_signal(
            barrier, inc=1, device_id=(lax.rem(dom + off, dom_size), hub), device_id_type=MESH
        )
    return barrier


def remote(src, dst, send, recv, dom, hub):
    return pltpu.make_async_remote_copy(
        src_ref=src,
        dst_ref=dst,
        send_sem=send,
        recv_sem=recv,
        device_id=(dom, hub),
        device_id_type=MESH,
    )


def exchange_kernel(
    dom_size,
    hub_size,
    local_ids,
    rows_hbm,
    counts_hbm,
    feats_hbm,
    hub_hbm,
    tiles_hbm,
    halo_ref,
    hub_all_ref,
    column_ref,
    local_sum_ref,
    rows_in,
    counts_in,
    feats,
    tiles,
    index,
    outgoing,
    load_sem,
    hub_send,
    hub_recv,
    relay_send,
    relay_recv,
    dom_send,
    dom_recv,
):
    dom = lax.axis_index("dom")
    hub = lax.axis_index("hub")
    blocks, tile, width = feats.shape
    row_count = blocks * tile
    hub_rows = hub_hbm.shape[0]
    cap = rows_in.shape[1]
    line = hub_size // 2
    core = lax.rem(hub, 2)
    place = hub // 2
    sibling = hub + 1 - 2 * core
    loads = [
        pltpu.make_async_copy(source, target, load_sem.at[number])
        for number, (source, target) in enumerate(
            (
                (rows_hbm, rows_in),
                (counts_hbm, counts_in),
                (feats_hbm, feats),
                (hub_hbm, hub_all_ref.at[rows_at(hub, hub_rows)]),
                (tiles_hbm, tiles),
            )
        )
    ]
    for load in loads:
        load.start()
    barrier = greet(dom_size, hub_size, dom, hub)
    pl.semaphore_wait(barrier, hub_size + dom_size - 2)
    own_block = hub_all_ref.at[rows_at(hub, hub_rows)]
    hub_copies = []
    for off in range(line):
        target = sibling if off == 0 else lax.rem(place + off, line) * 2 + core
        hub_copies.append(
            remote(hub_hbm, own_block, hub_send.at[off], hub_recv.at[off], dom, target)
        )
    for copy in hub_copies[1:] + hub_copies[:1]:
        copy.start()
    for load in loads[:3]:
        load.wait()
    shape = (dom_size, dom_size)
    diagonal = lax.broadcasted_iota(jnp.int32, shape, 0) == lax.broadcasted_iota(
        jnp.int32, shape, 1
    )
    wide_counts = jnp.broadcast_to(counts_in[...].astype(F32), shape)
    count = jnp.sum(jnp.where(diagonal, wide_counts, 0.0), axis=1, keepdims=True)
    live = lax.broadcasted_iota(jnp.int32, (dom_size, cap), 1).astype(F32) < count
    index[...] = jnp.full((128, 128), -1.0, F32)
    index[:dom_size, :cap] = jnp.where(live, rows_in[...].astype(F32), -1.0)
    turned = index[...].T
    column = jnp.concatenate(
        [
            jnp.broadcast_to(turned[:cap, peer : peer + 1], (cap, 128))
            for peer in range(dom_size)
        ],
        axis=0,
    )
    column_ref[...] = column
    lane = lax.broadcasted_iota(jnp.int32, column.shape, 1).astype(F32)
    onehot = jnp.concatenate(
        [
            (column == lane + float(start)).astype(F32).astype(BF16)
            for start in range(0, row_count, 128)
        ],
        axis=1,
    )
    outgoing[...] = jnp.dot(
        onehot, feats[...].reshape(row_count, width), preferred_element_type=F32).astype(BF16)
    dom_copies = []
    for off in range(1, dom_size):
        target = lax.rem(dom + off, dom_size)
        dom_copies.append(
            remote(
                outgoing.at[rows_at(target, cap)],
                halo_ref.at[rows_at(dom, cap)],
                dom_send.at[off],
                dom_recv.at[off],
                target,
                hub,
            )
        )
        dom_copies[-1].start()
    halo_ref[rows_at(dom, cap), :] = outgoing[rows_at(dom, cap), :]
    for load in loads[3:]:
        load.wait()

    def local_sum(block, carry):
        taken = [tiles[block, k] for k in range(tiles.shape[1])]
        sources = [feats[local_ids[k, 0, block]] for k in range(tiles.shape[1])]
        local_sum_ref[rows_at(block, 128), :] = jnp.dot(
            jnp.concatenate(taken, axis=1),
            jnp.concatenate(sources, axis=0),
            preferred_element_type=F32,
        )
        return carry

    lax.fori_loop(0, blocks // 2, local_sum, 0)
    relays = []
    for off in range(1, line):
        hub_copies[off].wait()
        source = hub_all_ref.at[
            rows_at(lax.rem(place + line - off, line) * 2 + core, hub_rows)
        ]
        relays.append(
            remote(source, source, relay_send.at[off], relay_recv.at[off], dom, sibling)
        )
        relays[-1].start()
    lax.fori_loop(blocks // 2, blocks, local_sum, 0)
    for copy in hub_copies[:1] + relays + dom_copies:
        copy.wait()


def layer_kernel(
    span,
    hub_size,
    weight_rows,
    local_ids,
    halo_ids,
    hub_ids,
    feats_ref,
    local_sum_ref,
    halo_ref,
    hub_ref,
    local_tiles,
    halo_tiles,
    hub_tiles,
    degree_ref,
    out_grad_ref,
    w_self_ref,
    w_neigh_ref,
    bias_ref,
    layer_ref,
    own_ref,
    halo_back_ref,
    payload_ref,
    bias_part_ref,
    halo_acc,
    hub_acc,
    weight_acc,
    bias_acc,
):
    step = pl.program_id(0)
    width = feats_ref.shape[1]

    @pl.when(step == 0)
    def _():
        own_ref[...] = jnp.zeros_like(own_ref)
        halo_acc[...] = jnp.zeros_like(halo_acc)
        hub_acc[...] = jnp.zeros_like(hub_acc)
        weight_acc[...] = jnp.zeros_like(weight_acc)
        bias_acc[...] = jnp.zeros_like(bias_acc)

    groups = (
        (lambda k, block: local_ids[k, 0, block], local_tiles, None, own_ref),
        (lambda k, block: halo_ids[k, block], halo_tiles, halo_ref, halo_acc),
        (lambda k, block: hub_ids[k, block], hub_tiles, hub_ref, hub_acc),
    )
    features = feats_ref[...]
    scales = []
    sums = []
    for sub in range(span):
        block = step * span + sub
        scale = 1.0 / degree_ref[pl.ds(block, 1), :].astype(F32)
        scale = jnp.broadcast_to(scale, (128, 128)).T
        scales.append(jnp.concatenate([scale] * (width // 128), axis=1))
        tiles = []
        sources = []
        for ids, tile_ref, source_ref, _ in groups[1:]:
            for k in range(tile_ref.shape[1]):
                tiles.append(tile_ref[sub, k])
                sources.append(source_ref[rows_at(ids(k, block), 128), :])
        total = local_sum_ref[sub * 128 : (sub + 1) * 128, :] + jnp.dot(
            jnp.concatenate(tiles, axis=1),
            jnp.concatenate(sources, axis=0),
            preferred_element_type=F32,
        )
        sums.append((total * scales[-1]).astype(BF16))
    aggregate = jnp.concatenate(sums, axis=0)
    preact = (
        jnp.dot(features, w_self_ref[...], preferred_element_type=F32)
        + jnp.dot(aggregate, w_neigh_ref[...], preferred_element_type=F32)
        + bias_ref[...]
    )
    sigmoid = 1.0 / (1.0 + jnp.exp(-preact))
    layer_ref[...] = (preact * sigmoid).astype(BF16)
    grad_wide = out_grad_ref[...].astype(F32) * (sigmoid * (1.0 + preact * (1.0 - sigmoid)))
    grad_pre = grad_wide.astype(BF16)
    bias_acc[...] += jnp.sum(
        grad_pre.astype(F32).reshape(span * 16, 8, width), axis=0
    )
    contract_rows = (((0,), (0,)), ((), ()))
    contract_cols = (((1,), (1,)), ((), ()))
    weight_acc[...] += lax.dot_general(
        jnp.concatenate([features, aggregate], axis=1),
        grad_pre,
        contract_rows,
        preferred_element_type=F32,
    )
    own_ref[rows_at(step, span * 128), :] += lax.dot_general(
        grad_pre, w_self_ref[...], contract_cols, preferred_element_type=F32
    )
    back = lax.dot_general(grad_pre, w_neigh_ref[...], contract_cols, preferred_element_type=F32)
    for sub in range(span):
        block = step * span + sub
        scaled = (back[sub * 128 : (sub + 1) * 128, :] * scales[sub]).astype(BF16)
        for ids, tile_ref, _, acc_ref in groups:
            for k in range(tile_ref.shape[1]):
                acc_ref[rows_at(ids(k, block), 128), :] += lax.dot_general(
                    tile_ref[sub, k], scaled, contract_rows, preferred_element_type=F32
                )

    @pl.when(step == pl.num_programs(0) - 1)
    def _():
        halo_back_ref[...] = halo_acc[...].astype(BF16)
        hub_rows = hub_acc.shape[0] // hub_size
        pieces, line, unit = payload_ref.shape[1:4]
        for peer in range(hub_size):
            for piece in range(pieces):
                first = piece * unit
                parts = []
                if first < weight_rows:
                    end = min(first + unit, weight_rows)
                    base = peer * weight_rows
                    parts.append(weight_acc[base + first : base + end, :])
                low = max(first - weight_rows, 0)
                high = min(first + unit - weight_rows, hub_rows)
                if low < high:
                    base = peer * hub_rows
                    parts.append(hub_acc[base + low : base + high, :])
                rest = unit - sum(part.shape[0] for part in parts)
                if rest:
                    parts.append(jnp.zeros((rest, width), F32))
                at = 0
                for part in parts:
                    payload_ref[peer % 2, piece, peer // 2, at : at + part.shape[0], :] = part
                    at += part.shape[0]
        bias_part_ref[...] = bias_acc[...]


def reduce_kernel(
    dom_size,
    hub_size,
    weight_rows,
    factor,
    column_ref,
    own_hbm,
    halo_back_ref,
    payload_hbm,
    bias_part_ref,
    feats_grad_ref,
    self_ref,
    neigh_ref,
    bias_out_ref,
    hub_out_ref,
    own,
    returned,
    mine,
    core_land,
    line_out,
    line_land,
    held,
    partial,
    dom_land,
    gathered,
    weights,
    bias_hub,
    bias_dom,
    load_sem,
    core_send,
    core_recv,
    line_send,
    line_recv,
    bias_hub_send,
    bias_hub_recv,
    back_send,
    back_recv,
    dom_send,
    dom_recv,
    bias_dom_send,
    bias_dom_recv,
    gather_send,
    gather_recv,
    weight_send,
    weight_recv,
    relay_send,
    relay_recv,
):
    dom = lax.axis_index("dom")
    hub = lax.axis_index("hub")
    slots = column_ref.shape[0]
    cap = slots // dom_size
    pieces, line, unit, width = mine.shape
    share = unit // dom_size
    core = lax.rem(hub, 2)
    place = hub // 2
    sibling = hub + 1 - 2 * core
    loads = [
        pltpu.make_async_copy(payload_hbm.at[core], mine, load_sem.at[0]),
        pltpu.make_async_copy(own_hbm, own, load_sem.at[1]),
    ]
    for load in loads:
        load.start()
    barrier = greet(dom_size, hub_size, dom, hub)
    bias_hub[hub] = bias_part_ref[...]
    returned[rows_at(dom, cap), :] = halo_back_ref[rows_at(dom, cap), :]
    pl.semaphore_wait(barrier, hub_size + dom_size - 2)

    core_copies = []
    for q in range(pieces):
        core_copies.append(
            remote(
                payload_hbm.at[1 - core, q],
                core_land.at[q],
                core_send.at[q],
                core_recv.at[q],
                dom,
                sibling,
            )
        )
        core_copies[-1].start()
    bias_copies = []
    for off in range(1, hub_size):
        bias_copies.append(
            remote(
                bias_part_ref,
                bias_hub.at[hub],
                bias_hub_send.at[off],
                bias_hub_recv.at[off],
                dom,
                lax.rem(hub + off, hub_size),
            )
        )
        bias_copies[-1].start()
    back_copies = []
    for off in range(1, dom_size):
        target = lax.rem(dom + off, dom_size)
        back_copies.append(
            remote(
                halo_back_ref.at[rows_at(target, cap)],
                returned.at[rows_at(dom, cap)],
                back_send.at[off],
                back_recv.at[off],
                target,
                hub,
            )
        )
        back_copies[-1].start()
    loads[0].wait()
    line_copies = []
    for q in range(pieces):
        core_copies[q].wait()
        line_copies.append([])
        for off in range(1, line):
            target = lax.rem(place + off, line)
            line_out[q, off] = (mine[q, target] + core_land[q, target]).astype(BF16)
            copy = remote(
                line_out.at[q, off],
                line_land.at[q, off],
                line_send.at[q, off],
                line_recv.at[q, off],
                dom,
                target * 2 + core,
            )
            copy.start()
            line_copies[q].append(copy)
    for copy in bias_copies:
        copy.wait()
    bias_total = bias_hub[0]
    for peer in range(1, hub_size):
        bias_total = bias_total + bias_hub[peer]
    bias_dom[dom] = bias_total
    bias_copies = []
    for off in range(1, dom_size):
        bias_copies.append(
            remote(
                bias_dom.at[dom],
                bias_dom.at[dom],
                bias_dom_send.at[off],
                bias_dom_recv.at[off],
                lax.rem(dom + off, dom_size),
                hub,
            )
        )
        bias_copies[-1].start()
    dom_copies = []
    for q in range(pieces):
        total = mine[q, place] + core_land[q, place]
        for copy in line_copies[q]:
            copy.wait()
        for off in range(1, line):
            total = total + line_land[q, off].astype(F32)
        held[q] = total
        partial[q] = total.astype(BF16)
        dom_copies.append([])
        for off in range(1, dom_size):
            target = lax.rem(dom + off, dom_size)
            copy = remote(
                partial.at[q, rows_at(target, share)],
                dom_land.at[q, off],
                dom_send.at[q, off],
                dom_recv.at[q, off],
                target,
                hub,
            )
            copy.start()
            dom_copies[q].append(copy)
    gather_copies = []
    for q in range(pieces):
        for copy in dom_copies[q]:
            copy.wait()
        total = held[q, rows_at(dom, share), :]
        for off in range(1, dom_size):
            total = total + dom_land[q, off].astype(F32)
        gathered[q, rows_at(dom, share), :] = total.astype(BF16)
        gather_copies.append([])
        for off in range(1, dom_size):
            copy = remote(
                gathered.at[q, rows_at(dom, share)],
                gathered.at[q, rows_at(dom, share)],
                gather_send.at[q, off],
                gather_recv.at[q, off],
                lax.rem(dom + off, dom_size),
                hub,
            )
            copy.start()
            gather_copies[q].append(copy)

    for copy in gather_copies[0]:
        copy.wait()
    weights[hub] = gathered[0, :weight_rows, :]
    weight_copies = []
    for off in range(line):
        weight_copies.append(
            remote(
                gathered.at[0, pl.ds(0, weight_rows)],
                weights.at[hub],
                weight_send.at[off],
                weight_recv.at[off],
                dom,
                sibling if off == 0 else lax.rem(place + off, line) * 2 + core,
            )
        )
    for copy in weight_copies[1:] + weight_copies[:1]:
        copy.start()

    for copy in back_copies + bias_copies:
        copy.wait()
    loads[1].wait()
    bias_total = bias_dom[0]
    for peer in range(1, dom_size):
        bias_total = bias_total + bias_dom[peer]
    bias_out_ref[...] = jnp.sum(bias_total, axis=0, keepdims=True) * factor
    row_count = own.shape[0]

    def add_back(step, carry):
        rows = rows_at(step, 256)
        lane = lax.broadcasted_iota(jnp.int32, (slots, 256), 1) + step * 256
        wanted = jnp.concatenate([column_ref[...]] * 2, axis=1)
        onehot = (wanted == lane.astype(F32)).astype(F32).astype(BF16)
        feats_grad_ref[rows, :] = (
            own[rows, :]
            + lax.dot_general(
                onehot,
                returned[...],
                (((0,), (0,)), ((), ())),
                preferred_element_type=F32,
            )
        ).astype(BF16)
        return carry

    lax.fori_loop(0, row_count // 512, add_back, 0)
    relays = []
    for off in range(1, line):
        weight_copies[off].wait()
        source = weights.at[lax.rem(place + line - off, line) * 2 + core]
        relays.append(
            remote(source, source, relay_send.at[off], relay_recv.at[off], dom, sibling)
        )
        relays[-1].start()
    lax.fori_loop(row_count // 512, row_count // 256, add_back, 0)

    for copies in gather_copies[1:]:
        for copy in copies:
            copy.wait()
    hub_rows = hub_out_ref.shape[0]
    for q in range(pieces):
        low = max(q * unit, weight_rows)
        high = min((q + 1) * unit, weight_rows + hub_rows)
        if low < high:
            hub_out_ref[low - weight_rows : high - weight_rows, :] = gathered[
                q, low - q * unit : high - q * unit, :
            ].astype(F32)
    for copy in weight_copies[:1] + relays:
        copy.wait()
    half = hub_size // 2
    self_ref[...] = weights[:half].reshape(width, width).astype(F32) * factor
    neigh_ref[...] = weights[half:].reshape(width, width).astype(F32) * factor


def body(
    node_feats,
    hub_feats,
    w_self,
    w_neigh,
    out_bias,
    send_rows,
    send_counts,
    local_ids,
    local_tiles,
    halo_ids,
    halo_tiles,
    hub_ids,
    hub_tiles,
    degree,
    out_grad,
):
    dom_size = lax.axis_size("dom")
    hub_size = lax.axis_size("hub")
    rows, width = node_feats.shape[2:]
    tile = local_tiles.shape[-1]
    blocks = rows // tile
    cap = send_rows.shape[-1]
    slots = dom_size * cap
    hub_rows = hub_feats.shape[0]
    features = node_feats.reshape(rows, width)
    dma = pltpu.SemaphoreType.DMA
    any_spec = pl.BlockSpec(memory_space=pl.ANY)
    counts = (local_tiles.shape[3], halo_tiles.shape[3], hub_tiles.shape[3])
    local_sets = local_tiles.reshape(blocks, counts[0], tile, tile)
    local_table = jnp.transpose(local_ids, (0, 3, 1, 2)).reshape(counts[0], 1, blocks)
    halo_table = jnp.transpose(halo_ids, (0, 1, 3, 2)).reshape(counts[1], blocks)
    hub_table = jnp.transpose(hub_ids, (0, 1, 3, 2)).reshape(counts[2], blocks)
    line = hub_size // 2

    halo, hub_all, column, local_sum = pl.pallas_call(
        functools.partial(exchange_kernel, dom_size, hub_size),
        out_shape=(
            jax.ShapeDtypeStruct((slots, width), BF16),
            jax.ShapeDtypeStruct((hub_size * hub_rows, width), BF16),
            jax.ShapeDtypeStruct((slots, 128), F32),
            jax.ShapeDtypeStruct((rows, width), F32),
        ),
        in_specs=[pl.BlockSpec(memory_space=pltpu.SMEM)] + [any_spec] * 5,
        out_specs=(VMEM_SPEC,) * 4,
        scratch_shapes=[
            pltpu.VMEM((dom_size, cap), jnp.int32),
            pltpu.VMEM((1, dom_size), jnp.int32),
            pltpu.VMEM((blocks, tile, width), BF16),
            pltpu.VMEM((blocks, counts[0], tile, tile), BF16),
            pltpu.VMEM((128, 128), F32),
            pltpu.VMEM((slots, width), BF16),
            dma((5,)),
            dma((line,)),
            dma((line,)),
            dma((line,)),
            dma((line,)),
            dma((dom_size,)),
            dma((dom_size,)),
        ],
        compiler_params=pltpu.CompilerParams(
            collective_id=0, has_side_effects=True, vmem_limit_bytes=VMEM_LIMIT
        ),
        name="exchange",
    )(
        local_table,
        send_rows.reshape(dom_size, cap),
        send_counts.reshape(1, dom_size),
        node_feats.reshape(blocks, tile, width),
        hub_feats,
        local_sets,
    )

    span = 2
    weight_rows = 2 * width // hub_size
    unit = 16 * dom_size
    pieces = (weight_rows + hub_rows + unit - 1) // unit
    whole = lambda *shape: pl.BlockSpec(shape, lambda i, *_: (0,) * len(shape))
    tiles = lambda count: pl.BlockSpec((span, count, tile, tile), lambda i, *_: (i, 0, 0, 0))
    moving = pl.BlockSpec((span * tile, width), lambda i, *_: (i, 0))
    layer_rows, own_grad, halo_back, payload, bias_part = pl.pallas_call(
        functools.partial(layer_kernel, span, hub_size, weight_rows),
        out_shape=(
            jax.ShapeDtypeStruct((rows, width), BF16),
            jax.ShapeDtypeStruct((rows, width), F32),
            jax.ShapeDtypeStruct((slots, width), BF16),
            jax.ShapeDtypeStruct((2, pieces, line, unit, width), F32),
            jax.ShapeDtypeStruct((8, width), F32),
        ),
        grid_spec=pltpu.PrefetchScalarGridSpec(
            num_scalar_prefetch=3,
            grid=(blocks // span,),
            in_specs=[
                moving,
                moving,
                whole(slots, width),
                whole(hub_size * hub_rows, width),
                tiles(counts[0]),
                tiles(counts[1]),
                tiles(counts[2]),
                whole(blocks, tile),
                moving,
                whole(width, width),
                whole(width, width),
                whole(1, width),
            ],
            out_specs=(
                moving,
                whole(rows, width),
                whole(slots, width),
                whole(2, pieces, line, unit, width),
                whole(8, width),
            ),
            scratch_shapes=[
                pltpu.VMEM((slots, width), F32),
                pltpu.VMEM((hub_size * hub_rows, width), F32),
                pltpu.VMEM((2 * width, width), F32),
                pltpu.VMEM((8, width), F32),
            ],
        ),
        compiler_params=pltpu.CompilerParams(vmem_limit_bytes=VMEM_LIMIT),
        name="layer",
    )(
        local_table,
        halo_table,
        hub_table,
        features,
        local_sum,
        halo,
        hub_all,
        local_sets,
        halo_tiles.reshape(blocks, counts[1], tile, tile),
        hub_tiles.reshape(blocks, counts[2], tile, tile),
        degree.reshape(blocks, tile),
        out_grad.reshape(rows, width),
        w_self,
        w_neigh,
        out_bias.reshape(1, width),
    )

    factor = 1.0 / math.sqrt(rows * dom_size * hub_size)
    share = unit // dom_size
    pairs = [dma((pieces,))] * 2 + [dma((pieces, line))] * 2 + [dma((hub_size,))] * 2
    pairs += [dma((dom_size,))] * 2 + [dma((pieces, dom_size))] * 2 + [dma((dom_size,))] * 2
    pairs += [dma((pieces, dom_size))] * 2 + [dma((line,))] * 4
    feats_grad, grad_self, grad_neigh, grad_bias, hub_grads = pl.pallas_call(
        functools.partial(reduce_kernel, dom_size, hub_size, weight_rows, factor),
        out_shape=(
            jax.ShapeDtypeStruct((rows, width), BF16),
            jax.ShapeDtypeStruct((width, width), F32),
            jax.ShapeDtypeStruct((width, width), F32),
            jax.ShapeDtypeStruct((1, width), F32),
            jax.ShapeDtypeStruct((hub_rows, width), F32),
        ),
        in_specs=[VMEM_SPEC, any_spec, VMEM_SPEC, any_spec, VMEM_SPEC],
        out_specs=(VMEM_SPEC,) * 5,
        scratch_shapes=[
            pltpu.VMEM((rows, width), F32),
            pltpu.VMEM((slots, width), BF16),
            pltpu.VMEM((pieces, line, unit, width), F32),
            pltpu.VMEM((pieces, line, unit, width), F32),
            pltpu.VMEM((pieces, line, unit, width), BF16),
            pltpu.VMEM((pieces, line, unit, width), BF16),
            pltpu.VMEM((pieces, unit, width), F32),
            pltpu.VMEM((pieces, unit, width), BF16),
            pltpu.VMEM((pieces, dom_size, share, width), BF16),
            pltpu.VMEM((pieces, unit, width), BF16),
            pltpu.VMEM((hub_size, weight_rows, width), BF16),
            pltpu.VMEM((hub_size, 8, width), F32),
            pltpu.VMEM((dom_size, 8, width), F32),
            dma((2,)),
        ]
        + pairs,
        compiler_params=pltpu.CompilerParams(
            collective_id=1, has_side_effects=True, vmem_limit_bytes=VMEM_LIMIT
        ),
        name="reduce",
    )(column, own_grad, halo_back, payload, bias_part)
    return (
        layer_rows.reshape(node_feats.shape),
        feats_grad.reshape(node_feats.shape),
        grad_self,
        grad_neigh,
        grad_bias.reshape(width),
        hub_grads,
    )


def solution(mesh):
    placed = (
        P("dom", "hub", None, None),
        P("hub", None),
        P(),
        P(),
        P(),
        P("dom", "hub", None, None),
        P("dom", "hub", None),
        P("dom", "hub", None, None),
        P("dom", "hub", None, None, None, None),
        P("dom", "hub", None, None),
        P("dom", "hub", None, None, None, None),
        P("dom", "hub", None, None),
        P("dom", "hub", None, None, None, None),
        P("dom", "hub", None),
        P("dom", "hub", None, None),
    )
    return jax.shard_map(
        body,
        mesh=mesh,
        in_specs=placed,
        out_specs=(
            P("dom", "hub", None, None),
            P("dom", "hub", None, None),
            P(),
            P(),
            P(),
            P("hub", None),
        ),
        check_vma=False,
    )
```

time: 75.9 us -> 59.9 us (0.79)
  local copies, waits for them, and re-layouts: 18.6 us -> 5.02 us
  Pallas kernels: 55.3 us -> 53.9 us
    unnamed x27 -> x13, local copies, waits for them, and re-layouts: 15.4 us -> 5.02 us
    pallas_call x1, Pallas kernels: 29 us -> 23.9 us  [body(): pl.pallas_call(functools.partial(reduce_kernel, dom_size, hub_size, weigh...]
    reshape x4 -> x0, local copies, waits for them, and re-layouts: 3.03 us -> none  [the longest x1 0.76 us: body(): send_rows.reshape(dom_size, cap)]
    pallas_call x1, Pallas kernels: 12.1 us -> 15 us  [body(): pl.pallas_call(functools.partial(exchange_kernel, dom_size, hub_size), ou...]
    pallas_call x1, Pallas kernels: 14.2 us -> 15.1 us  [body(): pl.pallas_call(functools.partial(layer_kernel, span, hub_size, weight_row...]
where the time goes in v2:
time: 59.9 us; the launch traced here: 59.6 us
  Pallas kernels  53.9 us (90%)
  local copies, waits for them, and re-layouts  5.02 us (8%)
  between operations  0.69 us (1%)
    pallas_call x1, Pallas kernels, body(): pl.pallas_call(functools.partial(reduce_kernel, dom_size, hub_size, weigh...  23.9 us
    pallas_call x1, Pallas kernels, body(): pl.pallas_call(functools.partial(layer_kernel, span, hub_size, weight_row...  15.1 us
    pallas_call x1, Pallas kernels, body(): pl.pallas_call(functools.partial(exchange_kernel, dom_size, hub_size), ou...  15 us
    unnamed x13, local copies, waits for them, and re-layouts  5.02 us

profile of v2, /device:TPU:0, one launch (start us, length us, event | category | flops | bytes accessed | tf_op | source)
XLA Modules:
  0.0 59.6 jit_solution(12158081376041515151)
XLA Ops:
  0.6 15.0 %exchange.1 = (bf16[256,256]{1,0:T(8,128)(2,1)}, bf16[1024,256]{1,0:T(8,128)(2,1)}, f32[256,128]{1,0:T(8,128)}, f32[2048,256]{1,0:T(8,128)}) custom-call(s32[3,1,16]{2,1,0:T(1,128)} %bitcast.31, s32[8,32]{1,0:T(8,128)} %bitcast.33, s32[1,8]{1,0:T(1,128)} %bitcast.38, bf16[16,128,256]{2,1,0:T(8,128)(2,1)} %bitcast.24, bf16[256,256]{1,0:T(8,128)(2,1)} %hub_hbm.1, ...), custom_call_target="tpu_custom_call" | custom-call | tf_op jit(solution)/shard_map/exchange/pallas_call | solution.py:604
  15.6 15.1 %layer.1 = (bf16[2048,256]{1,0:T(8,128)(2,1)}, f32[2048,256]{1,0:T(8,128)}, bf16[256,256]{1,0:T(8,128)(2,1)}, f32[2,3,2,128,256]{4,3,2,1,0:T(8,128)}, f32[8,256]{1,0:T(8,128)}) custom-call(s32[3,1,16]{2,1,0:T(1,128)} %bitcast.32, s32[2,16]{1,0:T(2,128)} %bitcast.34, s32[2,16]{1,0:T(2,128)} %bitcast.35, bf16[2048,256]{1,0:T(8,128)(2,1)} %bitcast.25, ...), custom_call_target="tpu_custom_call" | custom-call | tf_op jit(solution)/shard_map/layer/pallas_call | solution.py:649
  30.7 23.9 %reduce.1 = (bf16[2048,256]{1,0:T(8,128)(2,1)}, f32[256,256]{1,0:T(8,128)}, f32[256,256]{1,0:T(8,128)}, f32[1,256]{1,0:T(1,128)}, f32[256,256]{1,0:T(8,128)}) custom-call(f32[256,128]{1,0:T(8,128)} %get-tuple-element.24.column_ref, f32[2048,256]{1,0:T(8,128)} %get-tuple-element.25.own_hbm, bf16[256,256]{1,0:T(8,128)(2,1)} %get-tuple-element.26.halo_back_ref, ...), custom_call_target="tpu_custom_call" | custom-call | tf_op jit(solution)/shard_map/reduce/pallas_call | solution.py:714
  54.6 0.0 copy-start.2
  54.6 0.0 copy-start.1
  54.6 0.0 copy-start.3
  54.6 0.0 copy-start
  54.6 2.3 %copy.26 = bf16[1,1,2048,256]{3,2,1,0:T(8,128)(2,1)} copy(bf16[1,1,2048,256]{3,2,1,0:T(8,128)(2,1)} %bitcast.29) | data formatting | bytes 2097152
  56.9 0.0 copy-done.2
  56.9 0.7 %copy.27 = f32[256,256]{1,0:T(8,128)} copy(f32[256,256]{1,0:T(8,128)S(1)} %copy-done.2) | data formatting | bytes 524288
  57.7 0.0 copy-done.1
  57.7 0.7 %copy.28 = f32[256,256]{1,0:T(8,128)} copy(f32[256,256]{1,0:T(8,128)S(1)} %copy-done.1) | data formatting | bytes 524288
  58.4 0.0 copy-done.3
  58.4 0.6 copy.29
  58.9 0.0 copy-done
  58.9 0.7 %copy.30 = f32[256,256]{1,0:T(8,128)} copy(f32[256,256]{1,0:T(8,128)S(1)} %copy-done) | data formatting | bytes 524288
Async XLA Ops:
  54.6 2.4 %copy-start.2 = (f32[256,256]{1,0:T(8,128)S(1)}, f32[256,256]{1,0:T(8,128)}, u32[]{:S(2)}) copy-start(f32[256,256]{1,0:T(8,128)} %get-tuple-element.42) | copy-start | bytes 786436
  54.6 3.1 %copy-start.1 = (f32[256,256]{1,0:T(8,128)S(1)}, f32[256,256]{1,0:T(8,128)}, u32[]{:S(2)}) copy-start(f32[256,256]{1,0:T(8,128)} %get-tuple-element.43) | copy-start | bytes 786436
  54.6 3.8 %copy-start.3 = (f32[1,256]{1,0:T(1,128)S(1)}, f32[1,256]{1,0:T(1,128)}, u32[]{:S(2)}) copy-start(f32[1,256]{1,0:T(1,128)} %get-tuple-element.32) | copy-start | bytes 3076
  54.6 4.3 %copy-start = (f32[256,256]{1,0:T(8,128)S(1)}, f32[256,256]{1,0:T(8,128)}, u32[]{:S(2)}) copy-start(f32[256,256]{1,0:T(8,128)} %get-tuple-element.45) | copy-start | bytes 786436

commit v3 on v2

--- a/solution.py
+++ b/solution.py
@@ -124,7 +124,7 @@
         ],
         axis=0,
     )
-    column_ref[...] = column
+    column_ref[...] = column.T[:8, :]
     lane = lax.broadcasted_iota(jnp.int32, column.shape, 1).astype(F32)
     onehot = jnp.concatenate(
         [
@@ -310,19 +310,13 @@
     dom_size,
     hub_size,
     weight_rows,
-    factor,
-    column_ref,
-    own_hbm,
     halo_back_ref,
     payload_hbm,
     bias_part_ref,
-    feats_grad_ref,
-    self_ref,
-    neigh_ref,
+    returned,
+    weights,
+    gathered,
     bias_out_ref,
-    hub_out_ref,
-    own,
-    returned,
     mine,
     core_land,
     line_out,
@@ -330,8 +324,6 @@
     held,
     partial,
     dom_land,
-    gathered,
-    weights,
     bias_hub,
     bias_dom,
     load_sem,
@@ -356,19 +348,14 @@
 ):
     dom = lax.axis_index("dom")
     hub = lax.axis_index("hub")
-    slots = column_ref.shape[0]
-    cap = slots // dom_size
+    cap = returned.shape[0] // dom_size
     pieces, line, unit, width = mine.shape
     share = unit // dom_size
     core = lax.rem(hub, 2)
     place = hub // 2
     sibling = hub + 1 - 2 * core
-    loads = [
-        pltpu.make_async_copy(payload_hbm.at[core], mine, load_sem.at[0]),
-        pltpu.make_async_copy(own_hbm, own, load_sem.at[1]),
-    ]
-    for load in loads:
-        load.start()
+    load = pltpu.make_async_copy(payload_hbm.at[core], mine, load_sem)
+    load.start()
     barrier = greet(dom_size, hub_size, dom, hub)
     bias_hub[hub] = bias_part_ref[...]
     returned[rows_at(dom, cap), :] = halo_back_ref[rows_at(dom, cap), :]
@@ -414,7 +401,7 @@
             )
         )
         back_copies[-1].start()
-    loads[0].wait()
+    load.wait()
     line_copies = []
     for q in range(pieces):
         core_copies[q].wait()
@@ -514,30 +501,10 @@
 
     for copy in back_copies + bias_copies:
         copy.wait()
-    loads[1].wait()
     bias_total = bias_dom[0]
     for peer in range(1, dom_size):
         bias_total = bias_total + bias_dom[peer]
-    bias_out_ref[...] = jnp.sum(bias_total, axis=0, keepdims=True) * factor
-    row_count = own.shape[0]
-
-    def add_back(step, carry):
-        rows = rows_at(step, 256)
-        lane = lax.broadcasted_iota(jnp.int32, (slots, 256), 1) + step * 256
-        wanted = jnp.concatenate([column_ref[...]] * 2, axis=1)
-        onehot = (wanted == lane.astype(F32)).astype(F32).astype(BF16)
-        feats_grad_ref[rows, :] = (
-            own[rows, :]
-            + lax.dot_general(
-                onehot,
-                returned[...],
-                (((0,), (0,)), ((), ())),
-                preferred_element_type=F32,
-            )
-        ).astype(BF16)
-        return carry
-
-    lax.fori_loop(0, row_count // 512, add_back, 0)
+    bias_out_ref[...] = bias_total
     relays = []
     for off in range(1, line):
         weight_copies[off].wait()
@@ -546,24 +513,53 @@
             remote(source, source, relay_send.at[off], relay_recv.at[off], dom, sibling)
         )
         relays[-1].start()
-    lax.fori_loop(row_count // 512, row_count // 256, add_back, 0)
-
     for copies in gather_copies[1:]:
         for copy in copies:
             copy.wait()
-    hub_rows = hub_out_ref.shape[0]
-    for q in range(pieces):
-        low = max(q * unit, weight_rows)
-        high = min((q + 1) * unit, weight_rows + hub_rows)
-        if low < high:
-            hub_out_ref[low - weight_rows : high - weight_rows, :] = gathered[
-                q, low - q * unit : high - q * unit, :
-            ].astype(F32)
     for copy in weight_copies[:1] + relays:
         copy.wait()
-    half = hub_size // 2
-    self_ref[...] = weights[:half].reshape(width, width).astype(F32) * factor
-    neigh_ref[...] = weights[half:].reshape(width, width).astype(F32) * factor
+
+
+def finish_kernel(
+    weight_rows,
+    factor,
+    column_ref,
+    own_ref,
+    returned_ref,
+    weights_ref,
+    gathered_ref,
+    bias_ref,
+    feats_grad_ref,
+    self_ref,
+    neigh_ref,
+    bias_out_ref,
+    hub_out_ref,
+):
+    step = pl.program_id(0)
+    rows, width = own_ref.shape
+    slots = returned_ref.shape[0]
+
+    @pl.when(step == 0)
+    def _():
+        pieces, unit = gathered_ref.shape[:2]
+        hub_rows = hub_out_ref.shape[0]
+        for q in range(pieces):
+            low = max(q * unit, weight_rows)
+            high = min((q + 1) * unit, weight_rows + hub_rows)
+            if low < high:
+                hub_out_ref[low - weight_rows : high - weight_rows, :] = gathered_ref[
+                    q, low - q * unit : high - q * unit, :
+                ].astype(F32)
+        half = weights_ref.shape[0] // 2
+        self_ref[...] = weights_ref[:half].reshape(width, width).astype(F32) * factor
+        neigh_ref[...] = weights_ref[half:].reshape(width, width).astype(F32) * factor
+        bias_out_ref[...] = jnp.sum(bias_ref[...], axis=0, keepdims=True) * factor
+
+    row = lax.broadcasted_iota(jnp.int32, (rows, slots), 0) + step * rows
+    onehot = (row.astype(F32) == column_ref[0:1, :]).astype(F32).astype(BF16)
+    feats_grad_ref[...] = (
+        own_ref[...] + jnp.dot(onehot, returned_ref[...], preferred_element_type=F32)
+    ).astype(BF16)
 
 
 def body(
@@ -606,7 +602,7 @@
         out_shape=(
             jax.ShapeDtypeStruct((slots, width), BF16),
             jax.ShapeDtypeStruct((hub_size * hub_rows, width), BF16),
-            jax.ShapeDtypeStruct((slots, 128), F32),
+            jax.ShapeDtypeStruct((8, slots), F32),
             jax.ShapeDtypeStruct((rows, width), F32),
         ),
         in_specs=[pl.BlockSpec(memory_space=pltpu.SMEM)] + [any_spec] * 5,
@@ -639,7 +635,7 @@
         local_sets,
     )
 
-    span = 2
+    span = 4
     weight_rows = 2 * width // hub_size
     unit = 16 * dom_size
     pieces = (weight_rows + hub_rows + unit - 1) // unit
@@ -711,8 +707,40 @@
     pairs = [dma((pieces,))] * 2 + [dma((pieces, line))] * 2 + [dma((hub_size,))] * 2
     pairs += [dma((dom_size,))] * 2 + [dma((pieces, dom_size))] * 2 + [dma((dom_size,))] * 2
     pairs += [dma((pieces, dom_size))] * 2 + [dma((line,))] * 4
+    returned, weights, gathered, bias_sum = pl.pallas_call(
+        functools.partial(reduce_kernel, dom_size, hub_size, weight_rows),
+        out_shape=(
+            jax.ShapeDtypeStruct((slots, width), BF16),
+            jax.ShapeDtypeStruct((hub_size, weight_rows, width), BF16),
+            jax.ShapeDtypeStruct((pieces, unit, width), BF16),
+            jax.ShapeDtypeStruct((8, width), F32),
+        ),
+        in_specs=[VMEM_SPEC, any_spec, VMEM_SPEC],
+        out_specs=(VMEM_SPEC,) * 4,
+        scratch_shapes=[
+            pltpu.VMEM((pieces, line, unit, width), F32),
+            pltpu.VMEM((pieces, line, unit, width), F32),
+            pltpu.VMEM((pieces, line, unit, width), BF16),
+            pltpu.VMEM((pieces, line, unit, width), BF16),
+            pltpu.VMEM((pieces, unit, width), F32),
+            pltpu.VMEM((pieces, unit, width), BF16),
+            pltpu.VMEM((pieces, dom_size, share, width), BF16),
+            pltpu.VMEM((hub_size, 8, width), F32),
+            pltpu.VMEM((dom_size, 8, width), F32),
+            dma(()),
+        ]
+        + pairs,
+        compiler_params=pltpu.CompilerParams(
+            collective_id=1, has_side_effects=True, vmem_limit_bytes=VMEM_LIMIT
+        ),
+        name="reduce",
+    )(halo_back, payload, bias_part)
+
+    large = pl.BlockSpec((rows // 4, width), lambda i: (i, 0))
+    fixed = lambda *shape: pl.BlockSpec(shape, lambda i: (0,) * len(shape))
     feats_grad, grad_self, grad_neigh, grad_bias, hub_grads = pl.pallas_call(
-        functools.partial(reduce_kernel, dom_size, hub_size, weight_rows, factor),
+        functools.partial(finish_kernel, weight_rows, factor),
+        grid=(4,),
         out_shape=(
             jax.ShapeDtypeStruct((rows, width), BF16),
             jax.ShapeDtypeStruct((width, width), F32),
@@ -720,30 +748,24 @@
             jax.ShapeDtypeStruct((1, width), F32),
             jax.ShapeDtypeStruct((hub_rows, width), F32),
         ),
-        in_specs=[VMEM_SPEC, any_spec, VMEM_SPEC, any_spec, VMEM_SPEC],
-        out_specs=(VMEM_SPEC,) * 5,
-        scratch_shapes=[
-            pltpu.VMEM((rows, width), F32),
-            pltpu.VMEM((slots, width), BF16),
-            pltpu.VMEM((pieces, line, unit, width), F32),
-            pltpu.VMEM((pieces, line, unit, width), F32),
-            pltpu.VMEM((pieces, line, unit, width), BF16),
-            pltpu.VMEM((pieces, line, unit, width), BF16),
-            pltpu.VMEM((pieces, unit, width), F32),
-            pltpu.VMEM((pieces, unit, width), BF16),
-            pltpu.VMEM((pieces, dom_size, share, width), BF16),
-            pltpu.VMEM((pieces, unit, width), BF16),
-            pltpu.VMEM((hub_size, weight_rows, width), BF16),
-            pltpu.VMEM((hub_size, 8, width), F32),
-            pltpu.VMEM((dom_size, 8, width), F32),
-            dma((2,)),
-        ]
-        + pairs,
-        compiler_params=pltpu.CompilerParams(
-            collective_id=1, has_side_effects=True, vmem_limit_bytes=VMEM_LIMIT
+        in_specs=[
+            fixed(8, slots),
+            large,
+            fixed(slots, width),
+            fixed(hub_size, weight_rows, width),
+            fixed(pieces, unit, width),
+            fixed(8, width),
+        ],
+        out_specs=(
+            large,
+            fixed(width, width),
+            fixed(width, width),
+            fixed(1, width),
+            fixed(hub_rows, width),
         ),
-        name="reduce",
-    )(column, own_grad, halo_back, payload, bias_part)
+        compiler_params=pltpu.CompilerParams(vmem_limit_bytes=VMEM_LIMIT),
+        name="finish",
+    )(column, own_grad, returned, weights, gathered, bias_sum)
     return (
         layer_rows.reshape(node_feats.shape),
         feats_grad.reshape(node_feats.shape),

time: 59.9 us -> 55.8 us (0.932)
  local copies, waits for them, and re-layouts: 5.02 us -> 0 us
  Pallas kernels: 53.9 us -> 54.9 us
    unnamed x13 -> x0, local copies, waits for them, and re-layouts: 5.02 us -> none
    pallas_call x0 -> x1, Pallas kernels: none -> 4.3 us  [body(): pl.pallas_call(functools.partial(finish_kernel, weight_rows, factor), gri...]
    pallas_call x1, Pallas kernels: 15.1 us -> 12.3 us  [body(): pl.pallas_call(functools.partial(layer_kernel, span, hub_size, weight_row...]
where the time goes in v3:
time: 55.8 us; the launch traced here: 55.5 us
  Pallas kernels  54.9 us (98%)
  between operations  0.65 us (1%)
    pallas_call x1, Pallas kernels, body(): pl.pallas_call(functools.partial(reduce_kernel, dom_size, hub_size, weigh...  23.3 us
    pallas_call x1, Pallas kernels, body(): pl.pallas_call(functools.partial(exchange_kernel, dom_size, hub_size), ou...  15 us
    pallas_call x1, Pallas kernels, body(): pl.pallas_call(functools.partial(layer_kernel, span, hub_size, weight_row...  12.3 us
    pallas_call x1, Pallas kernels, body(): pl.pallas_call(functools.partial(finish_kernel, weight_rows, factor), gri...  4.3 us

profile of v3, /device:TPU:0, one launch (start us, length us, event | category | flops | bytes accessed | tf_op | source)
XLA Modules:
  0.0 55.5 jit_solution(5344762557819381897)
XLA Ops:
  0.6 15.0 %exchange.1 = (bf16[256,256]{1,0:T(8,128)(2,1)}, bf16[1024,256]{1,0:T(8,128)(2,1)}, f32[8,256]{1,0:T(8,128)}, f32[2048,256]{1,0:T(8,128)}) custom-call(s32[3,1,16]{2,1,0:T(1,128)} %bitcast.30, s32[8,32]{1,0:T(8,128)} %bitcast.32, s32[1,8]{1,0:T(1,128)} %bitcast.36, bf16[16,128,256]{2,1,0:T(8,128)(2,1)} %bitcast.24, bf16[256,256]{1,0:T(8,128)(2,1)} %hub_hbm.1, ...), custom_call_target="tpu_custom_call" | custom-call | tf_op jit(solution)/shard_map/exchange/pallas_call | solution.py:600
  15.6 12.3 %layer.1 = (bf16[2048,256]{1,0:T(8,128)(2,1)}, f32[2048,256]{1,0:T(8,128)}, bf16[256,256]{1,0:T(8,128)(2,1)}, f32[2,3,2,128,256]{4,3,2,1,0:T(8,128)}, f32[8,256]{1,0:T(8,128)}) custom-call(s32[3,1,16]{2,1,0:T(1,128)} %bitcast.31, s32[2,16]{1,0:T(2,128)} %bitcast.33, s32[2,16]{1,0:T(2,128)} %bitcast.34, bf16[2048,256]{1,0:T(8,128)(2,1)} %bitcast.25, ...), custom_call_target="tpu_custom_call" | custom-call | tf_op jit(solution)/shard_map/layer/pallas_call | solution.py:645
  27.9 23.3 %reduce.1 = (bf16[256,256]{1,0:T(8,128)(2,1)}, bf16[4,128,256]{2,1,0:T(8,128)(2,1)}, bf16[3,128,256]{2,1,0:T(8,128)(2,1)}, f32[8,256]{1,0:T(8,128)}) custom-call(bf16[256,256]{1,0:T(8,128)(2,1)} %get-tuple-element.30.halo_back_ref, f32[2,3,2,128,256]{4,3,2,1,0:T(8,128)} %get-tuple-element.31.payload_hbm, f32[8,256]{1,0:T(8,128)} %get-tuple-element.32.bias_part_ref), custom_call_target="tpu_custom_call" | custom-call | tf_op jit(solution)/shard_map/reduce/pallas_call | solution.py:710
  51.2 4.3 %finish.1 = (bf16[2048,256]{1,0:T(8,128)(2,1)}, f32[256,256]{1,0:T(8,128)}, f32[256,256]{1,0:T(8,128)}, f32[1,256]{1,0:T(1,128)}, f32[256,256]{1,0:T(8,128)}) custom-call(f32[8,256]{1,0:T(8,128)} %get-tuple-element.28.column_ref, f32[2048,256]{1,0:T(8,128)} %get-tuple-element.29.own_ref, bf16[256,256]{1,0:T(8,128)(2,1)} %get-tuple-element.33.returned_ref, ...), custom_call_target="tpu_custom_call" | custom-call | tf_op jit(solution)/shard_map/finish/pallas_call | solution.py:741

commit v4 on v3

--- a/solution.py
+++ b/solution.py
@@ -153,17 +153,19 @@
     for load in loads[3:]:
         load.wait()
 
-    def local_sum(block, carry):
-        taken = [tiles[block, k] for k in range(tiles.shape[1])]
-        sources = [feats[local_ids[k, 0, block]] for k in range(tiles.shape[1])]
-        local_sum_ref[rows_at(block, 128), :] = jnp.dot(
-            jnp.concatenate(taken, axis=1),
-            jnp.concatenate(sources, axis=0),
-            preferred_element_type=F32,
-        )
+    def local_sum(group, carry):
+        for sub in range(4):
+            block = group * 4 + sub
+            taken = [tiles[block, k] for k in range(tiles.shape[1])]
+            sources = [feats[local_ids[k, 0, block]] for k in range(tiles.shape[1])]
+            local_sum_ref[rows_at(block, 128), :] = jnp.dot(
+                jnp.concatenate(taken, axis=1),
+                jnp.concatenate(sources, axis=0),
+                preferred_element_type=F32,
+            )
         return carry
 
-    lax.fori_loop(0, blocks // 2, local_sum, 0)
+    lax.fori_loop(0, blocks // 8, local_sum, 0)
     relays = []
     for off in range(1, line):
         hub_copies[off].wait()
@@ -174,7 +176,7 @@
             remote(source, source, relay_send.at[off], relay_recv.at[off], dom, sibling)
         )
         relays[-1].start()
-    lax.fori_loop(blocks // 2, blocks, local_sum, 0)
+    lax.fori_loop(blocks // 8, blocks // 4, local_sum, 0)
     for copy in hub_copies[:1] + relays + dom_copies:
         copy.wait()
 
@@ -199,10 +201,11 @@
     w_neigh_ref,
     bias_ref,
     layer_ref,
-    own_ref,
+    own_out_ref,
     halo_back_ref,
     payload_ref,
     bias_part_ref,
+    own_ref,
     halo_acc,
     hub_acc,
     weight_acc,
@@ -280,6 +283,7 @@
 
     @pl.when(step == pl.num_programs(0) - 1)
     def _():
+        own_out_ref[...] = own_ref[...].astype(BF16)
         halo_back_ref[...] = halo_acc[...].astype(BF16)
         hub_rows = hub_acc.shape[0] // hub_size
         pieces, line, unit = payload_ref.shape[1:4]
@@ -301,7 +305,7 @@
                     parts.append(jnp.zeros((rest, width), F32))
                 at = 0
                 for part in parts:
-                    payload_ref[peer % 2, piece, peer // 2, at : at + part.shape[0], :] = part
+                    payload_ref[peer % 2, piece, peer // 2, at : at + part.shape[0], :] = part.astype(BF16)
                     at += part.shape[0]
         bias_part_ref[...] = bias_acc[...]
 
@@ -408,7 +412,9 @@
         line_copies.append([])
         for off in range(1, line):
             target = lax.rem(place + off, line)
-            line_out[q, off] = (mine[q, target] + core_land[q, target]).astype(BF16)
+            line_out[q, off] = (
+                mine[q, target].astype(F32) + core_land[q, target].astype(F32)
+            ).astype(BF16)
             copy = remote(
                 line_out.at[q, off],
                 line_land.at[q, off],
@@ -440,7 +446,7 @@
         bias_copies[-1].start()
     dom_copies = []
     for q in range(pieces):
-        total = mine[q, place] + core_land[q, place]
+        total = mine[q, place].astype(F32) + core_land[q, place].astype(F32)
         for copy in line_copies[q]:
             copy.wait()
         for off in range(1, line):
@@ -558,7 +564,7 @@
     row = lax.broadcasted_iota(jnp.int32, (rows, slots), 0) + step * rows
     onehot = (row.astype(F32) == column_ref[0:1, :]).astype(F32).astype(BF16)
     feats_grad_ref[...] = (
-        own_ref[...] + jnp.dot(onehot, returned_ref[...], preferred_element_type=F32)
+        own_ref[...].astype(F32) + jnp.dot(onehot, returned_ref[...], preferred_element_type=F32)
     ).astype(BF16)
 
 
@@ -646,9 +652,9 @@
         functools.partial(layer_kernel, span, hub_size, weight_rows),
         out_shape=(
             jax.ShapeDtypeStruct((rows, width), BF16),
-            jax.ShapeDtypeStruct((rows, width), F32),
+            jax.ShapeDtypeStruct((rows, width), BF16),
             jax.ShapeDtypeStruct((slots, width), BF16),
-            jax.ShapeDtypeStruct((2, pieces, line, unit, width), F32),
+            jax.ShapeDtypeStruct((2, pieces, line, unit, width), BF16),
             jax.ShapeDtypeStruct((8, width), F32),
         ),
         grid_spec=pltpu.PrefetchScalarGridSpec(
@@ -676,6 +682,7 @@
                 whole(8, width),
             ),
             scratch_shapes=[
+                pltpu.VMEM((rows, width), F32),
                 pltpu.VMEM((slots, width), F32),
                 pltpu.VMEM((hub_size * hub_rows, width), F32),
                 pltpu.VMEM((2 * width, width), F32),
@@ -718,8 +725,8 @@
         in_specs=[VMEM_SPEC, any_spec, VMEM_SPEC],
         out_specs=(VMEM_SPEC,) * 4,
         scratch_shapes=[
-            pltpu.VMEM((pieces, line, unit, width), F32),
-            pltpu.VMEM((pieces, line, unit, width), F32),
+            pltpu.VMEM((pieces, line, unit, width), BF16),
+            pltpu.VMEM((pieces, line, unit, width), BF16),
             pltpu.VMEM((pieces, line, unit, width), BF16),
             pltpu.VMEM((pieces, line, unit, width), BF16),
             pltpu.VMEM((pieces, unit, width), F32),

time: 55.8 us -> 54.9 us (0.984)
  Pallas kernels: 54.9 us -> 54 us
    pallas_call x1, Pallas kernels: 12.3 us -> 11.7 us  [body(): pl.pallas_call(functools.partial(layer_kernel, span, hub_size, weight_row...]
where the time goes in v4:
time: 54.9 us; the launch traced here: 54.7 us
  Pallas kernels  54 us (98%)
  between operations  0.65 us (1%)
    pallas_call x1, Pallas kernels, body(): pl.pallas_call(functools.partial(reduce_kernel, dom_size, hub_size, weigh...  23.7 us
    pallas_call x1, Pallas kernels, body(): pl.pallas_call(functools.partial(exchange_kernel, dom_size, hub_size), ou...  14.5 us
    pallas_call x1, Pallas kernels, body(): pl.pallas_call(functools.partial(layer_kernel, span, hub_size, weight_row...  11.7 us
    pallas_call x1, Pallas kernels, body(): pl.pallas_call(functools.partial(finish_kernel, weight_rows, factor), gri...  4.19 us

profile of v4, /device:TPU:0, one launch (start us, length us, event | category | flops | bytes accessed | tf_op | source)
XLA Modules:
  0.0 54.7 jit_solution(8033742338141905976)
XLA Ops:
  0.6 14.5 %exchange.1 = (bf16[256,256]{1,0:T(8,128)(2,1)}, bf16[1024,256]{1,0:T(8,128)(2,1)}, f32[8,256]{1,0:T(8,128)}, f32[2048,256]{1,0:T(8,128)}) custom-call(s32[3,1,16]{2,1,0:T(1,128)} %bitcast.30, s32[8,32]{1,0:T(8,128)} %bitcast.32, s32[1,8]{1,0:T(1,128)} %bitcast.36, bf16[16,128,256]{2,1,0:T(8,128)(2,1)} %bitcast.24, bf16[256,256]{1,0:T(8,128)(2,1)} %hub_hbm.1, ...), custom_call_target="tpu_custom_call" | custom-call | tf_op jit(solution)/shard_map/exchange/pallas_call | solution.py:606
  15.1 11.7 %layer.1 = (bf16[2048,256]{1,0:T(8,128)(2,1)}, bf16[2048,256]{1,0:T(8,128)(2,1)}, bf16[256,256]{1,0:T(8,128)(2,1)}, bf16[2,3,2,128,256]{4,3,2,1,0:T(8,128)(2,1)}, f32[8,256]{1,0:T(8,128)}) custom-call(s32[3,1,16]{2,1,0:T(1,128)} %bitcast.31, s32[2,16]{1,0:T(2,128)} %bitcast.33, s32[2,16]{1,0:T(2,128)} %bitcast.34, bf16[2048,256]{1,0:T(8,128)(2,1)} %bitcast.25, ...), custom_call_target="tpu_custom_call" | custom-call | tf_op jit(solution)/shard_map/layer/pallas_call | solution.py:651
  26.8 23.7 %reduce.1 = (bf16[256,256]{1,0:T(8,128)(2,1)}, bf16[4,128,256]{2,1,0:T(8,128)(2,1)}, bf16[3,128,256]{2,1,0:T(8,128)(2,1)}, f32[8,256]{1,0:T(8,128)}) custom-call(bf16[256,256]{1,0:T(8,128)(2,1)} %get-tuple-element.30.halo_back_ref, bf16[2,3,2,128,256]{4,3,2,1,0:T(8,128)(2,1)} %get-tuple-element.31.payload_hbm, f32[8,256]{1,0:T(8,128)} %get-tuple-element.32.bias_part_ref), custom_call_target="tpu_custom_call" | custom-call | tf_op jit(solution)/shard_map/reduce/pallas_call | solution.py:717
  50.5 4.2 %finish.1 = (bf16[2048,256]{1,0:T(8,128)(2,1)}, f32[256,256]{1,0:T(8,128)}, f32[256,256]{1,0:T(8,128)}, f32[1,256]{1,0:T(1,128)}, f32[256,256]{1,0:T(8,128)}) custom-call(f32[8,256]{1,0:T(8,128)} %get-tuple-element.28.column_ref, bf16[2048,256]{1,0:T(8,128)(2,1)} %get-tuple-element.29.own_ref, bf16[256,256]{1,0:T(8,128)(2,1)} %get-tuple-element.33.returned_ref, ...), custom_call_target="tpu_custom_call" | custom-call | tf_op jit(solution)/shard_map/finish/pallas_call | solution.py:748
